TPU v7x, 256 devices: a whole 4x4x8 slice. The times are simulated.
256 devices in a mesh: segment: 2 (over core), gx: 16 (over x, y), gy: 8 (over z).
Axes of the slice: x: 4, y: 4, z: 8, core: 2. Of those that a mesh axis runs over, the one named last changes fastest.
Arguments:
- volume: bfloat16 [4, 128, 512, 256], P(None, 'gx', 'gy'), may hold values from -6 to 6
- weight_high: bfloat16 [16, 4, 3, 3, 3], replicated, may hold values from -0.625 to 0.625
- bias_high: float32 [16], replicated, may hold values from -3 to 3
- weight_low: bfloat16 [32, 16, 3, 3, 3], replicated, may hold values from -0.3125 to 0.3125
- bias_low: float32 [32], replicated, may hold values from -3 to 3
- head_weight: float32 [32, 4], replicated, may hold values from -3 to 3
- head_bias: float32 [4], replicated, may hold values from -3 to 3
- targets: float32 [4], replicated, may hold values from -8 to 8
Outputs:
- predicted: float32 [4], replicated
- boundary_grad: bfloat16 [16, 64, 256, 128], P(None, 'gx', 'gy')
- grad_weight_high: float32 [16, 4, 3, 3, 3], replicated
- grad_bias_high: float32 [16], replicated
- grad_weight_low: float32 [32, 16, 3, 3, 3], replicated
- grad_bias_low: float32 [32], replicated
- grad_head: float32 [32, 4], replicated
All inputs are finite; a program needn't handle non-finite values.
Results may differ from a plain program's by a relative error of at most 0.0054.
Values may be sent and summed in bfloat16 or wider, within the bound.
A program may use at most 192 MiB of HBM per device.

v0:
```python
import jax
import jax.numpy as jnp
from jax import lax
from jax.sharding import PartitionSpec as P

layout_spec = ("NCDHW", "OIDHW", "NCDHW")


def shifted(array, axis, by):
    peers = lax.axis_size(axis)
    pairs = [(i, i + by) for i in range(peers) if 0 <= i + by < peers]
    return lax.ppermute(array, axis, pairs)


def as_sent(array):
    return jax.tree.map(lambda a: a.astype(jnp.bfloat16) if a.dtype == jnp.float32 else a, array)


def conv_down(widened, weight):
    return lax.conv_general_dilated(
        widened[None],
        weight,
        (2, 2, 2),
        "VALID",
        dimension_numbers=layout_spec,
        preferred_element_type=jnp.float32,
    )[0]


def weight_grad(widened, upstream):
    result = lax.conv_general_dilated(
        widened[:, None],
        upstream[:, None],
        (1, 1, 1),
        "VALID",
        rhs_dilation=(2, 2, 2),
        dimension_numbers=layout_spec,
        preferred_element_type=jnp.float32,
    )
    return jnp.transpose(result, (1, 0, 2, 3, 4))


def data_grad(upstream, weight):
    kernel = jnp.transpose(jnp.flip(weight, (2, 3, 4)), (1, 0, 2, 3, 4))
    return lax.conv_general_dilated(
        upstream[None],
        kernel,
        (1, 1, 1),
        ((2, 2), (2, 2), (2, 2)),
        lhs_dilation=(2, 2, 2),
        dimension_numbers=layout_spec,
        preferred_element_type=jnp.float32,
    )[0]


def silu_slope(values):
    sigmoid_part = jax.nn.sigmoid(values)
    return sigmoid_part * (1.0 + values * (1.0 - sigmoid_part))


def lower_rims(block):
    below_x = shifted(block[:, -1:], "gx", 1)
    wider = jnp.concatenate([below_x, block], axis=1)
    below_y = shifted(wider[:, :, -1:], "gy", 1)
    return jnp.concatenate([below_y, wider], axis=2)


def return_rims(widened):
    from_above = shifted(as_sent(widened[:, :1]), "gx", -1)
    inner = widened[:, 1:]
    inner = inner.at[:, -1:].add(from_above)
    from_side = shifted(as_sent(inner[:, :, :1]), "gy", -1)
    inner = inner[:, :, 1:]
    return inner.at[:, :, -1:].add(from_side)


def shards(volume, weight_high, bias_high, weight_low, bias_low, head_weight, head_bias, targets):
    in_chans, cells_x, cells_y, depth_all = volume.shape
    mid_chans = weight_high.shape[0]
    low_chans = weight_low.shape[0]
    half_x = cells_x // 2
    half_y = cells_y // 2
    padded = jnp.pad(lower_rims(volume), ((0, 0), (0, 0), (0, 0), (1, 0)))
    pieces = 1
    slab_depth = depth_all // pieces
    half_depth = slab_depth // 2
    quarter_depth = slab_depth // 4
    on_high = lax.axis_index("segment") == 0
    empty_pre_high = jnp.zeros((mid_chans, half_x, half_y, half_depth), jnp.float32)
    empty_act = jnp.zeros((mid_chans, half_x, half_y, half_depth), jnp.bfloat16)
    empty_pre_low = jnp.zeros((low_chans, cells_x // 4, cells_y // 4, quarter_depth), jnp.float32)
    empty_sum = jnp.zeros((low_chans,), jnp.float32)

    def high_slab():
        return padded

    pre_high_list = []
    pre_low_list = []
    widened_list = []
    pooled_part = empty_sum
    carry_plane = jnp.zeros((mid_chans, half_x + 1, half_y + 1, 1), jnp.bfloat16)
    incoming = None
    for moment in range(pieces + 1):
        run_high = moment < pieces
        run_low = moment >= 1

        def high_work(index=moment):
            pre_high = conv_down(high_slab(), weight_high) + bias_high[:, None, None, None]
            return (pre_high, jax.nn.silu(pre_high).astype(jnp.bfloat16))

        def low_work(source=incoming):
            pre_low = conv_down(source, weight_low) + bias_low[:, None, None, None]
            return (pre_low, jnp.sum(jax.nn.silu(pre_low), axis=(1, 2, 3)))

        if run_high:
            pre_high, act_high = lax.cond(on_high, high_work, lambda: (empty_pre_high, empty_act))
        else:
            pre_low, partial_value = lax.cond(on_high, lambda: (empty_pre_low, empty_sum), low_work)
        if run_high:
            pre_high_list.append(pre_high)
        if run_low:
            pre_low_list.append(pre_low)
            widened_list.append(incoming)
            pooled_part = pooled_part + partial_value
        if run_high:
            arrived = lower_rims(shifted(act_high, "segment", 1))
            incoming = jnp.concatenate([carry_plane, arrived], axis=3)
            carry_plane = arrived[..., -1:]
    total = lax.psum(pooled_part, ("segment", "gx", "gy"))
    low_cells = (
        cells_x // 4 * lax.axis_size("gx") * (cells_y // 4 * lax.axis_size("gy")) * (depth_all // 4)
    )
    pooled = total / low_cells
    predicted = jnp.dot(pooled, head_weight, precision=lax.Precision.HIGHEST) + head_bias
    error = predicted - targets
    grad_head = pooled[:, None] * error[None, :]
    signal = jnp.dot(head_weight, error, precision=lax.Precision.HIGHEST)
    grad_w_high = jnp.zeros((mid_chans, in_chans, 3, 3, 3), jnp.float32)
    grad_b_high = jnp.zeros((mid_chans,), jnp.float32)
    grad_w_low = jnp.zeros((low_chans, mid_chans, 3, 3, 3), jnp.float32)
    grad_b_low = jnp.zeros((low_chans,), jnp.float32)
    empty_spread = jnp.zeros((mid_chans, half_x + 1, half_y + 1, half_depth + 1), jnp.float32)
    depth_carry = jnp.zeros((mid_chans, half_x, half_y, 1), jnp.float32)
    boundary_slabs = [None] * pieces
    received = None
    for moment in range(pieces + 1):
        run_low = moment < pieces
        run_high = moment >= 1
        low_index = pieces - 1 - moment
        high_index = pieces - moment

        def low_back(index=low_index):
            up_low = (signal[:, None, None, None] * silu_slope(pre_low_list[index])).astype(
                jnp.bfloat16
            )
            return (
                data_grad(up_low, weight_low),
                weight_grad(widened_list[index], up_low),
                jnp.sum(up_low.astype(jnp.float32), axis=(1, 2, 3)),
            )

        def high_back(index=high_index, source=received):
            up_high = (source.astype(jnp.float32) * silu_slope(pre_high_list[index])).astype(
                jnp.bfloat16
            )
            return (
                weight_grad(high_slab(), up_high),
                jnp.sum(up_high.astype(jnp.float32), axis=(1, 2, 3)),
            )

        if run_low:
            spread, part_w_low, part_b_low = lax.cond(
                on_high, lambda: (empty_spread, grad_w_low * 0.0, grad_b_low * 0.0), low_back
            )
        else:
            part_w_high, part_b_high = lax.cond(
                on_high, high_back, lambda: (grad_w_high * 0.0, grad_b_high * 0.0)
            )
        if run_high:
            grad_w_high = grad_w_high + part_w_high
            grad_b_high = grad_b_high + part_b_high
        if run_low:
            grad_w_low = grad_w_low + part_w_low
            grad_b_low = grad_b_low + part_b_low
            settled = return_rims(spread)
            upper = settled[..., 1:]
            upper = upper.at[..., -1:].add(depth_carry)
            depth_carry = settled[..., :1]
            grad_slab = upper.astype(jnp.bfloat16)
            received = shifted(grad_slab, "segment", -1)
            boundary_slabs[low_index] = jnp.where(on_high, received, grad_slab)
    boundary_grad = jnp.concatenate(boundary_slabs, axis=3)
    sum_w_high, sum_b_high, sum_w_low, sum_b_low = lax.psum(
        (grad_w_high, grad_b_high, grad_w_low, grad_b_low), ("segment", "gx", "gy")
    )
    return (
        predicted,
        boundary_grad,
        sum_w_high / low_cells,
        sum_b_high / low_cells,
        sum_w_low / low_cells,
        sum_b_low / low_cells,
        grad_head,
    )


def solution(mesh):
    placed = (P(None, "gx", "gy", None), P(), P(), P(), P(), P(), P(), P())
    return jax.shard_map(
        shards,
        mesh=mesh,
        in_specs=placed,
        out_specs=(P(), P(None, "gx", "gy", None), P(), P(), P(), P(), P()),
        check_vma=False,
    )
```

profile of v0, /device:TPU:1, one launch (start us, length us, event | category | flops | bytes accessed | tf_op | source)
XLA Modules:
  0.0 755.1 jit_solution(17205192526251947410)
XLA Ops:
  0.7 0.9 slice.117
  1.6 4.0 collective-permute-start
  5.6 2.1 collective-permute-done
  7.8 1.3 pad_maximum_fusion
  9.1 0.9 copy.122
  10.1 3.5 collective-permute-start.1
  13.6 0.9 collective-permute-done.1
  14.5 1.5 fusion.44
  16.0 4.3 conditional.4
  16.0 2.5 broadcast_in_dim.11
  18.5 1.7 broadcast_in_dim.16
  20.4 2.6 copy.125
  23.0 1.3 collective-permute-start.2
  24.3 81.7 %collective-permute-done.2 = bf16[16,4,32,128]{3,2,1,0:T(8,128)(2,1)S(1)} collective-permute-done((bf16[16,4,32,128]{3,2,1,0:T(8,128)(2,1)S(1)}, bf16[16,4,32,128]{3,2,1,0:T(8,128)(2,1)S(1)}, u32[]{:S(2)}, u32[]{:S(2)}) %collective-permute-start.2) | collective-permute-done | bytes 524320 | tf_op jit(solution)/shard_map/ppermute | solution.py:12
  106.0 4.1 collective-permute-start.3
  110.1 2.7 collective-permute-done.3
  113.0 3.9 collective-permute-start.4
  116.9 0.3 copy.127
  117.2 0.8 collective-permute-done.4
  118.0 0.5 fusion.45
  118.6 25.7 %conditional.5 = (f32[32,2,16,64]{0,2,3,1:T(8,128)}, f32[32]{0:T(128)S(1)}) conditional(s32[]{:T(128)} %convert_element_type.37, (bf16[16,5,33,129]{3,0,2,1:T(8,128)(2,1)S(1)}, bf16[32,16,3,3,3]{0,1,4,3,2:T(8,128)(2,1)S(1)}, f32[32]{0:T(128)S(1)}) %tuple.94, () %tuple.55), branch_computations={%region_2.4_spmd, %region_4.5_spmd} | conditional | flops 66702304 | bytes 6743734 | solution.py:118
  119.0 4.4 copy.128
  123.4 3.9 pad.14
  127.3 8.4 %copy.113 = bf16[16,5,33,1,8,18]{0,4,5,2,1,3:T(8,128)(2,1)} copy(bf16[16,5,33,1,8,18]{2,0,5,4,1,3:T(8,128)(2,1)} %bitcast.69) | data formatting | bytes 1520640 | tf_op jit(solution)/shard_map/cond/branch_0_fun/conv_general_dilated | solution.py:20
  135.7 1.3 slice.136
  137.1 5.7 fusion.18
  142.8 0.2 copy.114
  143.0 1.2 multiply_reduce_fusion
  144.3 83.7 %psum.35 = f32[32]{0:T(128)S(1)} all-reduce(f32[32]{0:T(128)S(1)} %get-tuple-element.92), channel_id=1, replica_groups=mesh['segment'=2,'gx'=16,'gy'=8] {'segment','gx','gy'}, use_global_device_ids=true, to_apply=%region_5.6 | all-reduce | flops 32 | bytes 256 | tf_op jit(solution)/shard_map/psum | solution.py:129
  228.0 0.6 fusion.51
  228.8 73.5 %conditional.6 = (f32[16,5,33,129]{2,0,3,1:T(8,128)}, f32[32,16,3,3,3]{0,1,4,3,2:T(8,128)}, f32[32]{0:T(128)S(1)}) conditional(s32[]{:T(128)} %convert_element_type.37, (f32[32]{0:T(128)S(1)}, f32[32,2,16,64]{0,2,3,1:T(8,128)}, bf16[32,16,3,3,3]{0,1,4,3,2:T(8,128)(2,1)S(1)}, bf16[16,5,33,129]{3,0,2,1:T(8,128)(2,1)S(1)}) %tuple.95, () %tuple.57), branch_computations={%region_6.8_spmd, %region_8.9_spmd} | conditional | flops 121916640 | bytes 11225638 | solution.py:172
  228.8 1.7 convert_reduce_fusion
  230.6 0.2 copy.116
  230.8 0.5 copy-done.3
  231.3 11.8 %broadcast_select_fusion.1 = f32[5,33,8,18,16]{4,2,3,1,0:T(8,128)} fusion(pred[8,18]{0,1:T(8,128)(4,1)} %constant.148, bf16[32,16,3,3,3]{0,1,4,3,2:T(8,128)(2,1)S(1)} %get-tuple-element.70, bf16[32,2,16,1,7,1]{0,4,5,2,1,3:T(8,128)(2,1)S(1)} %slice.138, bf16[32,2,16,1,8,9]{0,4,5,2,1,3:T(8,128)(2,1)S(1)} %copy.116), kind=kOutput, calls=%fused_computation.26 | convolution fusion | flops 64572672 | bytes 1710224 | tf_op jit(solution)/shard_map/cond/branch_0_fun/conv_general_dilated | solution.py:45
  243.1 10.4 %copy.117 = f32[5,33,8,18,16]{1,4,3,2,0:T(8,128)} copy(f32[5,33,8,18,16]{4,2,3,1,0:T(8,128)} %broadcast_select_fusion.1) | data formatting | bytes 3041280 | tf_op jit(solution)/shard_map/cond/branch_0_fun/conv_general_dilated | solution.py:45
  253.5 5.2 slice_bitcast_fusion.2
  258.6 18.0 %copy.118 = bf16[16,1,5,33,129]{0,1,4,3,2:T(2,128)(2,1)} copy(bf16[16,1,5,33,129]{4,0,3,2,1:T(8,128)(2,1)S(1)} %bitcast.68) | data formatting | bytes 1362240 | tf_op jit(solution)/shard_map/cond/branch_0_fun/broadcast_in_dim | solution.py:32
  276.7 25.7 %fusion.26 = f32[32,16,3,3,3]{0,1,4,3,2:T(8,128)} fusion(bf16[16,1,5,33,129]{0,1,4,3,2:T(2,128)(2,1)} %copy.118, bf16[32,1,2,16,64]{0,3,4,2,1:T(8,128)(2,1)} %bitcast.77), kind=kOutput, calls=%fused_computation.32 | convolution fusion | flops 56623104 | bytes 867488 | tf_op jit(solution)/shard_map/cond/branch_0_fun/transpose | solution.py:40
  302.3 6.7 copy.131
  309.1 1.1 slice.161
  310.2 1.3 collective-permute-start.5
  311.5 6.8 copy.130
  318.3 1.3 slice_add_fusion
  319.6 0.6 slice-done
  320.2 0.3 copy_dynamic-update-slice_fusion
  320.6 1.5 collective-permute-start.6
  322.0 0.4 slice.146
  322.4 3.4 collective-permute-done.6
  326.0 0.9 scatter-add.11
  327.0 1.0 slice.149
  328.0 7.3 scatter-add.14
  335.3 1.3 collective-permute-start.7
  336.6 0.6 broadcast_multiply_fusion.2
  337.3 1.0 collective-permute-done.7
  338.3 1.1 conditional.7
  338.3 0.6 broadcast.80
  339.0 0.5 broadcast.81
  339.5 412.2 %all-reduce.2 = (f32[16,4,3,3,3]{0,1,4,3,2:T(4,128)S(1)}, f32[16]{0:T(128)S(1)}, f32[32,16,3,3,3]{0,1,4,3,2:T(8,128)S(1)}, f32[32]{0:T(128)S(1)}) all-reduce(f32[16,4,3,3,3]{0,1,4,3,2:T(4,128)} %get-tuple-element.96, f32[16]{0:T(128)} %get-tuple-element.97, ...), channel_id=1, replica_groups=mesh['segment'=2,'gx'=16,'gy'=8] {'segment','gx','gy'}, use_global_device_ids=true, to_apply=%region_12.13 | all-reduce | flops 15600 | bytes 124800 | tf_op jit(solution)/shard_map/psum | solution.py:193
  751.7 0.7 broadcast_multiply_fusion
  752.4 0.6 broadcast_multiply_fusion.1
  753.0 0.5 broadcast_multiply_fusion.3
  753.5 0.5 broadcast_multiply_fusion.4
  754.1 0.8 broadcast_select_fusion.2
  (40 shorter events, 0.7 us)
Async XLA Ops:
  0.6 227.4 %copy-start = (f32[32,4]{0,1:T(4,128)S(1)}, f32[32,4]{0,1:T(4,128)}, u32[]{:S(2)}) copy-start(f32[32,4]{0,1:T(4,128)} %param.27) | copy-start | bytes 1540
  0.6 15.4 %copy-start.9 = (bf16[16,4,3,3,3]{0,1,4,3,2:T(4,128)(2,1)S(1)}, bf16[16,4,3,3,3]{0,1,4,3,2:T(4,128)(2,1)}, u32[]{:S(2)}) copy-start(bf16[16,4,3,3,3]{0,1,4,3,2:T(4,128)(2,1)} %param.23) | copy-start | bytes 10372
  0.7 15.4 %copy-start.7 = (f32[16]{0:T(128)S(1)}, f32[16]{0:T(128)}, u32[]{:S(2)}) copy-start(f32[16]{0:T(128)} %param.24) | copy-start | bytes 196
  1.6 6.2 collective-permute-start
  10.1 4.4 collective-permute-start.1
  20.4 98.2 %copy-start.6 = (f32[32]{0:T(128)S(1)}, f32[32]{0:T(128)}, u32[]{:S(2)}) copy-start(f32[32]{0:T(128)} %param.26) | copy-start | bytes 388
  20.4 98.2 %copy-start.8 = (bf16[32,16,3,3,3]{0,1,4,3,2:T(8,128)(2,1)S(1)}, bf16[32,16,3,3,3]{0,1,4,3,2:T(8,128)(2,1)}, u32[]{:S(2)}) copy-start(bf16[32,16,3,3,3]{0,1,4,3,2:T(8,128)(2,1)} %param.25) | copy-start | bytes 82948
  23.0 83.0 %collective-permute-start.2 = (bf16[16,4,32,128]{3,2,1,0:T(8,128)(2,1)S(1)}, bf16[16,4,32,128]{3,2,1,0:T(8,128)(2,1)S(1)}, u32[]{:S(2)}, u32[]{:S(2)}) collective-permute-start(bf16[16,4,32,128]{3,2,1,0:T(8,128)(2,1)S(1)} %copy.125), channel_id=1, source_target_pairs={{0,128},{1,129},{2,130},{3,131},{4,132},{5,133},{6,134},{7,135},{8... | collective-permute-start | bytes 1572872 | tf_op jit(solution)/shard_map/ppermute | solution.py:12
  106.0 6.9 collective-permute-start.3
  113.0 5.0 collective-permute-start.4
  118.6 109.4 %copy-start.10 = (f32[4]{0:T(128)S(1)}, f32[4]{0:T(128)}, u32[]{:S(2)}) copy-start(f32[4]{0:T(128)} %param.29) | copy-start | bytes 52
  118.6 109.4 %copy-start.11 = (f32[4]{0:T(128)S(1)}, f32[4]{0:T(128)}, u32[]{:S(2)}) copy-start(f32[4]{0:T(128)} %param.28) | copy-start | bytes 52
  127.3 9.7 %copy-start.13 = (pred[8,9]{0,1:T(8,128)(4,1)S(1)}, pred[8,9]{0,1:T(8,128)(4,1)}, u32[]{:S(2)}) copy-start(pred[8,9]{0,1:T(8,128)(4,1)} %constant.149) | copy-start | bytes 220 | tf_op jit(solution)/shard_map/cond
  230.5 0.8 copy-start.3
  302.3 7.8 %copy-start.4 = (f32[32]{0:T(128)}, f32[32]{0:T(128)S(1)}, u32[]{:S(2)}) copy-start(f32[32]{0:T(128)S(1)} %get-tuple-element.99) | copy-start | bytes 388
  310.2 8.1 %collective-permute-start.5 = (bf16[16,1,33,129]{3,0,2,1:T(8,128)(2,1)S(1)}, bf16[16,1,33,129]{3,0,2,1:T(8,128)(2,1)S(1)}, u32[]{:S(2)}, u32[]{:S(2)}) collective-permute-start(bf16[16,1,33,129]{3,0,2,1:T(8,128)(2,1)S(1)} %slice.161), channel_id=1, source_target_pairs={{8,0},{16,8},{24,16},{32,24},{40,32},{48,40},{56,48},{64,56},{72,6... | collective-permute-start | bytes 408680 | tf_op jit(solution)/shard_map/ppermute | solution.py:12
  318.3 1.9 slice-start
  320.6 5.3 collective-permute-start.6
  335.3 3.0 collective-permute-start.7
  338.3 1.1 copy-start.5
  338.3 415.7 %copy-start.2 = (bf16[16,4,32,128]{3,2,1,0:T(8,128)(2,1)S(1)}, bf16[16,4,32,128]{3,2,1,0:T(8,128)(2,1)}, u32[]{:S(2)}) copy-start(bf16[16,4,32,128]{3,2,1,0:T(8,128)(2,1)} %scatter-add.14) | copy-start | bytes 1572868
  339.5 415.4 %copy-start.1 = (f32[32,4]{0,1:T(4,128)S(1)}, f32[32,4]{0,1:T(4,128)}, u32[]{:S(2)}) copy-start(f32[32,4]{0,1:T(4,128)} %param.27) | copy-start | bytes 1540
where the time goes:
time: 766 us; the launch traced here: 755 us
  blocking collectives  496 us (65%)
  waiting for transfers between devices  92.7 us (12%)
  local copies, waits for them, and re-layouts  88.2 us (12%)
  matrix products  44 us (6%)
  starting transfers between devices  21 us (3%)
  other arithmetic  11.5 us (2%)
    psum x1, blocking collectives, shards(): lax.psum((grad_w_high, grad_b_high, grad_w_low, grad_b_low), ('segment',...  412 us
    ppermute x8, waiting for transfers between devices, shifted(): return lax.ppermute(array, axis, pairs)  92.7 us
    psum x1, blocking collectives, shards(): total = lax.psum(pooled_part, ('segment', 'gx', 'gy'))  83.7 us
    transpose x1, matrix products, weight_grad(): return jnp.transpose(result, (1, 0, 2, 3, 4))  25.7 us
    ppermute x8, starting transfers between devices, shifted(): return lax.ppermute(array, axis, pairs)  21 us
    broadcast_in_dim x1, local copies, waits for them, and re-layouts, weight_grad(): widened[:, None]  18 us
  transfers between devices with their start and end apart: 8, of which 7 were waited for; matrix products, arithmetic and copies ran while one was open for 1% of the time, Pallas kernels for 0%

commit v1 on v0

v1 whole, which is shorter than its diff:
```python
import functools

import jax
import jax.numpy as jnp
import numpy as np
from jax import lax
from jax.experimental import pallas as pl
from jax.experimental.pallas import tpu as pltpu
from jax.sharding import PartitionSpec as P

MESH = pl.DeviceIdType.MESH
BF = jnp.bfloat16
F32 = jnp.float32


def depth_taps():
    z = np.arange(256)[:, None, None]
    k = np.arange(3)[None, :, None]
    p = np.arange(128)[None, None, :]
    return (z == 2 * p + k - 1).reshape(256, 384)


def rows_to_channels():
    out = np.zeros((16, 16, 12, 16), bool)
    for r in range(12):
        for y in range(16):
            out[y, r, r, y] = True
    return out.reshape(256, 192)


def depth_taps_low():
    out = np.zeros((2, 128, 3, 2, 64), bool)
    for h in range(2):
        for k in range(3):
            for p in range(64):
                if 2 * p + k - 1 >= 0:
                    out[h, 2 * p + k - 1, k, h, p] = True
    return out.reshape(256, 384)


def depth_spread():
    out = np.zeros((2, 64, 2, 3, 128), bool)
    for h in range(2):
        for k in range(3):
            for p in range(64):
                if 2 * p + k - 1 >= 0:
                    out[h, p, h, k, 2 * p + k - 1] = True
    return out.reshape(128, 768)


def channels_to_rows():
    out = np.zeros((16, 16, 16, 16), bool)
    for i in range(16):
        for y in range(16):
            out[i, y, y, i] = True
    return out.reshape(256, 256)


def mm(a, b):
    return lax.dot_general(a, b, (((1,), (0,)), ((), ())), preferred_element_type=F32)


def mm_nt(a, b):
    return lax.dot_general(a, b, (((1,), (1,)), ((), ())), preferred_element_type=F32)


def kernel(
    nx, ny, cells,
    v, w1, b1, wl, bl, hw, hb, tg, wb, s1, p1, s2, e1, p2,
    bg_out, pred_out, head_out, grad_out,
    halo, a1, pre, act, taps, slope, slope_y, up, grad_b,
    pool_s, pool_1, pool_2, gsend, g_1, g_2s, g_2, g_3,
    hs, hr, p1s, p1r, p2s, p2r, g1s, g1r, g2s, g2r, g3s, g3r,
):
    mx = lax.axis_index("gx")
    my = lax.axis_index("gy")
    xu, xd = lax.rem(mx + 1, nx), lax.rem(mx + nx - 1, nx)
    yu, yd = lax.rem(my + 1, ny), lax.rem(my + ny - 1, ny)

    barrier = pltpu.get_barrier_semaphore()
    partners = [{"gx": lax.rem(mx + d, nx)} for d in range(1, nx)]
    partners += [{"gy": lax.rem(my + d, ny)} for d in range(1, ny)]
    partners += [{"gx": xu, "gy": yu}, {"gx": xd, "gy": yd}]
    for peer in partners:
        pl.semaphore_signal(barrier, inc=1, device_id=peer, device_id_type=MESH)
    pl.semaphore_wait(barrier, len(partners))

    def send(n, src, dst, peer):
        copy = pltpu.make_async_remote_copy(
            src_ref=src, dst_ref=dst, send_sem=hs.at[n], recv_sem=hr.at[n],
            device_id=peer, device_id_type=MESH,
        )
        copy.start()
        return copy

    copies = []
    c_raw = send(0, v.at[:, 7], halo, {"gx": xu})
    copies.append(c_raw)

    def to_channels(load, xs, yb):
        parts = []
        for h in range(2):
            raw = load(yb * 2 + h).reshape(64, 256)
            d = mm(raw, s1[...]).astype(BF)
            parts.append(jnp.concatenate([d[:, 0:128], d[:, 128:256], d[:, 256:384]], axis=0))
        out = mm(p1[...], jnp.concatenate(parts, axis=1)).astype(BF)
        for h in range(2):
            start = pl.multiple_of(16 + (yb * 2 + h) * 256, 16)
            a1[xs, pl.ds(start, 256), :] = out[:, h * 128:(h + 1) * 128]

    def own_plane(t, carry):
        x, yb = t // 2, lax.rem(t, 2)

        def load(b):
            return v[:, x, pl.ds(pl.multiple_of(b * 16, 16), 16), :]

        to_channels(load, x + 1, yb)
        return carry

    lax.fori_loop(0, 16, own_plane, 0)

    c_a1y = send(1, a1.at[pl.ds(1, 8), pl.ds(1024, 16)], a1.at[pl.ds(1, 8), pl.ds(0, 16)], {"gy": yu})
    c_a1c = send(2, a1.at[8, pl.ds(1024, 16)], a1.at[0, pl.ds(0, 16)], {"gx": xu, "gy": yu})
    copies += [c_a1y, c_a1c]

    c_raw.wait_recv()

    @pl.when(mx == 0)
    def _():
        halo[...] = jnp.zeros_like(halo)

    def halo_plane(yb, carry):
        def load(b):
            return halo[:, pl.ds(pl.multiple_of(b * 16, 16), 16), :]

        to_channels(load, 0, yb)
        return carry

    lax.fori_loop(0, 2, halo_plane, 0)
    c_a1y.wait_recv()
    c_a1c.wait_recv()

    @pl.when(my == 0)
    def _():
        a1[:, pl.ds(0, 16), :] = jnp.zeros((9, 16, 128), BF)

    @pl.when(mx == 0)
    def _():
        a1[0, pl.ds(0, 16), :] = jnp.zeros((16, 128), BF)

    def conv_high(t, carry):
        xp, yp = t // 16, lax.rem(t, 16)
        cols = []
        for h in range(2):
            px = xp * 2 + h
            start = pl.multiple_of(yp * 64, 16)
            cols.append(jnp.concatenate([a1[2 * px + k, pl.ds(start, 80), :] for k in range(3)], axis=0))
        out = mm(w1[...], jnp.concatenate(cols, axis=1)) + b1[...]
        sig = jax.nn.sigmoid(out)
        acts = (out * sig).astype(BF)
        for h in range(2):
            px = xp * 2 + h
            pre[px, pl.ds(pl.multiple_of(yp * 32, 32), 32), :] = out[:, h * 128:(h + 1) * 128]
            act[px + 1, pl.ds(pl.multiple_of(16 + yp * 32, 16), 32), :] = acts[:, h * 128:(h + 1) * 128]
        return carry

    lax.fori_loop(0, 32, conv_high, 0)

    c_ax = send(3, act.at[4, pl.ds(16, 512)], act.at[0, pl.ds(16, 512)], {"gx": xu})
    c_ay = send(4, act.at[pl.ds(1, 4), pl.ds(512, 16)], act.at[pl.ds(1, 4), pl.ds(0, 16)], {"gy": yu})
    c_ac = send(5, act.at[4, pl.ds(512, 16)], act.at[0, pl.ds(0, 16)], {"gx": xu, "gy": yu})
    copies += [c_ax, c_ay, c_ac]
    c_ax.wait_recv()
    c_ay.wait_recv()
    c_ac.wait_recv()

    @pl.when(mx == 0)
    def _():
        act[0] = jnp.zeros((528, 128), BF)

    @pl.when(my == 0)
    def _():
        act[:, pl.ds(0, 16), :] = jnp.zeros((5, 16, 128), BF)

    def to_taps(xs, carry):
        for first, count in ((0, 4), (4, 4), (8, 4), (12, 5)):
            low = act[xs, 16 * first:16 * (first + count), :]
            high = act[xs, 256 + 16 * first:256 + 16 * (first + count), :]
            d = mm(jnp.concatenate([low, high], axis=1), s2[...]).astype(BF)
            for t in range(count):
                for k in range(3):
                    row = ((first + t) * 3 + k) * 16
                    taps[xs, row:row + 16, :] = d[16 * t:16 * (t + 1), 128 * k:128 * (k + 1)]
        return carry

    lax.fori_loop(0, 5, to_taps, 0)

    def window(px, j):
        start = pl.multiple_of(j * 96, 16)
        return jnp.concatenate([taps[2 * px + k, pl.ds(start, 144), :] for k in range(3)], axis=0)

    def conv_low(j, total):
        out = mm(wl[...], jnp.concatenate([window(0, j), window(1, j)], axis=1)) + bl[...]
        sig = jax.nn.sigmoid(out)
        slopes = sig * (1.0 + out * (1.0 - sig))
        values = out * sig
        for px in range(2):
            slope[px, pl.ds(pl.multiple_of(j * 32, 32), 32), :] = slopes[:, px * 128:(px + 1) * 128]
        return total + values[:, :128] + values[:, 128:]

    total = lax.fori_loop(0, 8, conv_low, jnp.zeros((32, 128), F32))

    c_sx = send(6, slope.at[0], slope.at[2], {"gx": xd})
    c_sy = send(7, slope.at[pl.ds(0, 2), pl.ds(0, 32)], slope_y.at[pl.ds(0, 2)], {"gy": yd})
    c_sc = send(8, slope.at[0, pl.ds(0, 32)], slope_y.at[2], {"gx": xd, "gy": yd})
    copies += [c_sx, c_sy, c_sc]

    lane = lax.broadcasted_iota(jnp.int32, (32, 128), 1)
    row = lax.broadcasted_iota(jnp.int32, (32, 128), 0)
    sums = jnp.sum(total, axis=1, keepdims=True)
    flat = jnp.sum(jnp.where(lane == row, sums, 0.0), axis=0, keepdims=True)
    mine = jnp.broadcast_to(flat, (8, 128))

    def exchange(axis, me, n, buffer, source, ssem, rsem):
        out = []
        for d in range(1, n):
            peer = lax.rem(me + d, n)
            copy = pltpu.make_async_remote_copy(
                src_ref=source(peer), dst_ref=buffer.at[me], send_sem=ssem.at[peer], recv_sem=rsem.at[me],
                device_id={axis: peer}, device_id_type=MESH,
            )
            copy.start()
            out.append(copy)
        return out

    def arrive(me, n, buffer, rsem):
        for d in range(1, n):
            peer = lax.rem(me + d, n)
            pltpu.make_async_copy(buffer.at[peer], buffer.at[peer], rsem.at[peer]).wait()

    pool_s[0] = mine
    pool_1[mx] = mine
    copies += exchange("gx", mx, nx, pool_1, lambda peer: pool_s.at[0], p1s, p1r)

    def slope_high(t, carry):
        px, yp = t // 8, lax.rem(t, 8)
        at = pl.ds(pl.multiple_of(yp * 64, 64), 64)
        val = pre[px, at, :]
        sig = jax.nn.sigmoid(val)
        pre[px, at, :] = sig * (1.0 + val * (1.0 - sig))
        return carry

    lax.fori_loop(0, 32, slope_high, 0)

    arrive(mx, nx, pool_1, p1r)
    part = pool_1[0]
    for d in range(1, nx):
        part = part + pool_1[d]
    pool_s[1] = part
    pool_2[my] = part
    copies += exchange("gy", my, ny, pool_2, lambda peer: pool_s.at[1], p2s, p2r)
    arrive(my, ny, pool_2, p2r)
    part = pool_2[0]
    for d in range(1, ny):
        part = part + pool_2[d]
    pooled = jnp.sum(jnp.where(lane == row, part[0:1, :], 0.0), axis=1, keepdims=True) * (1.0 / cells)
    weight = hw[...]
    predicted = jnp.sum(pooled * weight, axis=0, keepdims=True) + hb[...]
    error = predicted - tg[...]
    pred_out[...] = predicted
    head_out[...] = pooled * error
    signal = jnp.sum(weight * error, axis=1, keepdims=True)

    c_sx.wait_recv()
    c_sy.wait_recv()
    c_sc.wait_recv()

    @pl.when(mx == nx - 1)
    def _():
        slope[2] = jnp.zeros((256, 128), F32)
        slope_y[2] = jnp.zeros((32, 128), F32)

    @pl.when(my == ny - 1)
    def _():
        slope_y[...] = jnp.zeros((3, 32, 128), F32)

    def low_back(j, carry):
        g, gb = carry
        for px in range(3):
            f = signal * slope[px, pl.ds(pl.multiple_of(j * 32, 32), 32), :]
            u = f.astype(BF)
            if px < 2:
                g = g + mm_nt(u, window(px, j))
                gb = gb + u.astype(F32)
            d = mm(u, e1[...]).astype(BF)
            for h in range(2):
                for k in range(3):
                    start = pl.multiple_of(((8 * h + j) * 3 + k) * 32, 32)
                    col = (h * 3 + k) * 128
                    up[px, pl.ds(start, 32), :] = d[:, col:col + 128]
        return g, gb

    g_low, gb_low = lax.fori_loop(0, 8, low_back, (jnp.zeros((32, 432), F32), jnp.zeros((32, 128), F32)))
    for px in range(3):
        u = (signal * slope_y[px]).astype(BF)
        d = mm(u, e1[:, 0:384]).astype(BF)
        for k in range(3):
            up[px, (48 + k) * 32:(49 + k) * 32, :] = d[:, k * 128:(k + 1) * 128]

    def high_back(t, carry):
        g, gb = carry
        ax, ay = t // 16, lax.rem(t, 16)
        start = pl.multiple_of(ay * 96, 32)
        rhs = jnp.concatenate([up[ax, pl.ds(start, 192), :], up[ax + 1, pl.ds(start, 192), :]], axis=0)
        out = mm(wb[...], rhs).astype(BF)
        at = pl.ds(pl.multiple_of(ay * 32, 32), 32)
        ws, ups = [], []
        for sx in range(2):
            qx = 2 * ax + sx
            tile = out[32 * sx:32 * (sx + 1), :]
            grad_b[qx, at, :] = tile
            u = (tile.astype(F32) * pre[qx, at, :]).astype(BF)
            gb = gb + u.astype(F32)
            ups.append(u)
            begin = pl.multiple_of(ay * 64, 16)
            ws.append(jnp.concatenate([a1[2 * qx + k, pl.ds(begin, 80), :] for k in range(3)], axis=0))
        g = g + mm_nt(jnp.concatenate(ups, axis=1), jnp.concatenate(ws, axis=1))
        return g, gb

    g_high, gb_high = lax.fori_loop(0, 32, high_back, (jnp.zeros((32, 240), F32), jnp.zeros((32, 128), F32)))

    scale = 1.0 / cells
    pieces = []
    for k in range(3):
        pieces.append(g_high[0:16, k * 80:k * 80 + 48] + g_high[16:32, k * 80 + 32:k * 80 + 80])
    g_w = jnp.concatenate(pieces, axis=1)
    halves = jnp.concatenate([g_w[:, 0:72], g_w[:, 72:144]], axis=0)
    bias_low = jnp.sum(gb_low, axis=1, keepdims=True)
    bias_high = jnp.sum(gb_high, axis=1, keepdims=True)
    last = jnp.concatenate(
        [g_low[:, 384:432], halves, bias_low, bias_high, jnp.zeros((32, 6), F32)], axis=1
    )
    blocks = [g_low[:, 0:128], g_low[:, 128:256], g_low[:, 256:384], last]
    for b in range(4):
        for c in range(4):
            gsend[b * 4 + c] = blocks[c][8 * b:8 * (b + 1), :] * scale

    per = 16 // nx
    g_1[mx] = gsend[pl.ds(mx * per, per)]
    copies += exchange("gx", mx, nx, g_1, lambda peer: gsend.at[pl.ds(peer * per, per)], g1s, g1r)

    def place(t, carry):
        qx = t // 2
        h = lax.rem(t, 2)
        block = grad_b[qx, pl.ds(pl.multiple_of(h * 256, 256), 256), :]
        out = mm(p2[...], block).astype(BF).reshape(16, 16, 128)
        bg_out[:, qx, pl.ds(pl.multiple_of(h * 16, 16), 16), :] = out
        return carry

    lax.fori_loop(0, 8, place, 0)

    arrive(mx, nx, g_1, g1r)
    part = g_1[0]
    for d in range(1, nx):
        part = part + g_1[d]
    g_2s[...] = part
    g_2[my] = part
    copies += exchange("gy", my, ny, g_2, lambda peer: g_2s, g2s, g2r)
    arrive(my, ny, g_2, g2r)
    part = g_2[0]
    for d in range(1, ny):
        part = part + g_2[d]
    g_3[mx] = part
    copies += exchange("gx", mx, nx, g_3, lambda peer: g_3.at[mx], g3s, g3r)
    arrive(mx, nx, g_3, g3r)
    for d in range(nx):
        grad_out[pl.ds(d * per, per)] = g_3[d]
    for copy in copies:
        copy.wait_send()


def shards(nx, ny, volume, weight_high, bias_high, weight_low, bias_low, head_weight, head_bias, targets):
    cells = 2 * nx * 16 * ny * 64
    wh = jnp.transpose(weight_high, (0, 2, 3, 4, 1))
    wh = jnp.pad(wh, ((0, 0), (0, 0), (0, 0), (0, 1), (0, 0))).reshape(16, 3, 3, 16)
    w1 = jnp.concatenate(
        [
            jnp.pad(wh, ((0, 0), (0, 0), (0, 2), (0, 0))).reshape(16, 240),
            jnp.pad(wh, ((0, 0), (0, 0), (2, 0), (0, 0))).reshape(16, 240),
        ],
        axis=0,
    )
    wl = jnp.transpose(weight_low, (0, 2, 3, 4, 1)).reshape(32, 432)
    wt = jnp.transpose(weight_low, (1, 2, 3, 4, 0))
    wt = jnp.pad(wt, ((0, 0), (0, 1), (0, 1), (0, 0), (0, 0)))
    tap = ((1, 3), (2, 0))
    wb = jnp.stack(
        [
            jnp.stack([wt[:, tap[sx][dx], tap[sy][dy]] for dx in range(2) for dy in range(2)], axis=1)
            for sx in range(2)
            for sy in range(2)
        ],
        axis=0,
    ).reshape(64, 384)
    b1 = jnp.concatenate([bias_high, bias_high])[:, None]
    tables = [jnp.asarray(t().astype(np.float32), BF) for t in (depth_taps, rows_to_channels, depth_taps_low, depth_spread, channels_to_rows)]
    vm = pl.BlockSpec(memory_space=pltpu.VMEM)
    dma = pltpu.SemaphoreType.DMA
    per = 16 // nx
    bg, pred, head, grads = pl.pallas_call(
        functools.partial(kernel, nx, ny, cells),
        out_shape=(
            jax.ShapeDtypeStruct((16, 4, 32, 128), BF),
            jax.ShapeDtypeStruct((1, 4), F32),
            jax.ShapeDtypeStruct((32, 4), F32),
            jax.ShapeDtypeStruct((16, 8, 128), F32),
        ),
        in_specs=[vm] * 14,
        out_specs=(vm,) * 4,
        scratch_shapes=[
            pltpu.VMEM((4, 64, 256), BF),
            pltpu.VMEM((9, 1040, 128), BF),
            pltpu.VMEM((4, 512, 128), F32),
            pltpu.VMEM((5, 528, 128), BF),
            pltpu.VMEM((5, 816, 128), BF),
            pltpu.VMEM((3, 256, 128), F32),
            pltpu.VMEM((3, 32, 128), F32),
            pltpu.VMEM((3, 1632, 128), BF),
            pltpu.VMEM((4, 512, 128), BF),
            pltpu.VMEM((2, 8, 128), F32),
            pltpu.VMEM((nx, 8, 128), F32),
            pltpu.VMEM((ny, 8, 128), F32),
            pltpu.VMEM((16, 8, 128), F32),
            pltpu.VMEM((nx, per, 8, 128), F32),
            pltpu.VMEM((per, 8, 128), F32),
            pltpu.VMEM((ny, per, 8, 128), F32),
            pltpu.VMEM((nx, per, 8, 128), F32),
            dma((9,)), dma((9,)),
            dma((nx,)), dma((nx,)), dma((ny,)), dma((ny,)),
            dma((nx,)), dma((nx,)), dma((ny,)), dma((ny,)), dma((nx,)), dma((nx,)),
        ],
        compiler_params=pltpu.CompilerParams(
            collective_id=0, has_side_effects=True, vmem_limit_bytes=48 << 20
        ),
        name="fused",
    )(
        volume, w1, b1, wl, bias_low[:, None], head_weight, head_bias[None], targets[None], wb, *tables
    )
    g = grads.reshape(4, 4, 8, 128).transpose(0, 2, 1, 3).reshape(32, 512)
    g_low = g[:, :432].reshape(32, 27, 16).transpose(0, 2, 1).reshape(32, 16, 3, 3, 3)
    g_high = jnp.concatenate([g[:16, 432:504], g[16:, 432:504]], axis=1).reshape(16, 3, 3, 4, 4)[:, :, :, :3]
    g_high = g_high.transpose(0, 4, 1, 2, 3)
    gb_low = g[:, 504]
    gb_high = g[:16, 505] + g[16:, 505]
    return pred[0], bg, g_high, gb_high, g_low, gb_low, head


def solution(mesh):
    nx, ny = mesh.shape["gx"], mesh.shape["gy"]
    placed = (P(None, "gx", "gy", None), P(), P(), P(), P(), P(), P(), P())
    return jax.shard_map(
        functools.partial(shards, nx, ny),
        mesh=mesh,
        in_specs=placed,
        out_specs=(P(), P(None, "gx", "gy", None), P(), P(), P(), P(), P()),
        check_vma=False,
    )
```

time: 766 us -> 79.6 us (0.10)
  the two profiles are of different devices: /device:TPU:1 before, /device:TPU:8 now
where the time goes in v1:
time: 79.6 us; the launch traced here: 79.4 us
  Pallas kernels  70.3 us (88%)
  local copies, waits for them, and re-layouts  7.34 us (9%)
  other arithmetic  0.95 us (1%)
  between operations  0.82 us (1%)
    pallas_call x1, Pallas kernels, shards(): pl.pallas_call(functools.partial(kernel, nx, ny, cells), out_shape=(jax.S...  70.3 us
    unnamed x28, local copies, waits for them, and re-layouts  3.29 us

profile of v1, /device:TPU:8, one launch (start us, length us, event | category | flops | bytes accessed | tf_op | source)
XLA Modules:
  0.0 79.4 jit_solution(10007020425166820838)
XLA Ops:
  0.6 0.8 pad.14
  1.4 0.1 copy.39
  1.5 0.1 fusion.6
  1.6 0.0 copy-start.11
  1.6 0.0 copy-start.8
  1.6 0.0 copy-start.10
  1.6 0.0 copy-start.9
  1.6 0.1 reshape.47
  1.7 0.0 copy-start
  1.8 0.1 reshape.46
  1.9 0.4 copy-done.11
  2.2 0.1 maximum_bitcast_fusion.1
  2.3 0.1 copy.42.b1
  2.4 0.1 copy-done.8
  2.5 0.1 copy.43.wl
  2.6 0.0 copy-done.10
  2.6 0.1 copy.44.bl
  2.7 0.0 copy-done.9
  2.7 0.1 copy.45.hw
  2.8 0.0 copy-start.5
  2.9 0.1 pad_maximum_fusion
  2.9 0.0 copy-start.2
  2.9 0.0 copy-start.3
  2.9 0.0 copy-start.4
  3.0 0.1 copy.41
  3.1 0.0 copy-start.1
  3.1 0.0 copy-start.6
  3.1 0.0 copy-start.7
  3.1 0.2 reshape.49.wb
  3.3 0.0 copy-done
  3.3 0.5 copy-done.5
  3.8 0.1 copy-done.2
  3.9 0.1 copy-done.3
  3.9 0.0 copy-done.4
  4.0 0.1 copy-done.1
  4.0 0.0 copy-done.6
  4.1 0.0 copy-done.7
  4.1 70.3 %fused.1 = (bf16[16,4,32,128]{3,2,1,0:T(8,128)(2,1)S(1)}, f32[1,4]{1,0:T(1,128)S(1)}, f32[32,4]{1,0:T(8,128)S(1)}, f32[16,8,128]{2,1,0:T(8,128)S(1)}) custom-call(bf16[4,8,64,256]{3,2,1,0:T(8,128)(2,1)S(1)} %copy-done, bf16[32,240]{1,0:T(8,128)(2,1)S(1)} %pad_maximum_fusion.8.w1, f32[32,1]{1,0:T(8,128)S(1)} %copy.42.b1, bf16[32,432]{1,0:T(8,128)(2,1)S(1)} %copy.43.wl, ...), custom_call_target="tpu_custom_call" | custom-call | tf_op jit(solution)/shard_map/fused/pallas_call | solution.py:410
  74.3 0.1 fusion.5
  74.4 0.1 pad_maximum_fusion.9
  74.5 0.1 copy.46
  74.6 0.6 slice_bitcast_fusion
  75.2 0.7 fusion.4
  75.9 0.8 %copy.47 = f32[32,432]{0,1:T(8,128)} copy(f32[32,432]{1,0:T(8,128)S(1)} %bitcast.54) | data formatting | bytes 110592 | tf_op jit(solution)/shard_map/slice | solution.py:450
  76.8 0.7 slice_reduce_fusion
  77.4 0.7 copy.48
  78.1 0.5 copy.51
  78.6 0.8 copy.52
  (4 shorter events, 0.1 us)
Async XLA Ops:
  1.6 0.7 copy-start.11
  1.6 0.9 %copy-start.8 = (bf16[32,16,3,3,3]{0,1,4,3,2:T(8,128)(2,1)S(1)}, bf16[32,16,3,3,3]{0,1,4,3,2:T(8,128)(2,1)}, u32[]{:S(2)}) copy-start(bf16[32,16,3,3,3]{0,1,4,3,2:T(8,128)(2,1)} %param.16) | copy-start | bytes 82948
  1.6 1.0 %copy-start.10 = (f32[32]{0:T(128)S(1)}, f32[32]{0:T(128)}, u32[]{:S(2)}) copy-start(f32[32]{0:T(128)} %param.17) | copy-start | bytes 388
  1.6 1.1 %copy-start.9 = (f32[32,4]{0,1:T(4,128)S(1)}, f32[32,4]{0,1:T(4,128)}, u32[]{:S(2)}) copy-start(f32[32,4]{0,1:T(4,128)} %param.18) | copy-start | bytes 1540
  1.7 1.6 %copy-start = (bf16[4,8,64,256]{3,2,1,0:T(8,128)(2,1)S(1)}, bf16[4,8,64,256]{3,2,1,0:T(8,128)(2,1)}, u32[]{:S(2)}) copy-start(bf16[4,8,64,256]{3,2,1,0:T(8,128)(2,1)} %v.1) | copy-start | bytes 3145732
  2.8 0.9 %copy-start.5 = (bf16[256,256]{1,0:T(8,128)(2,1)S(1)}, bf16[256,256]{1,0:T(8,128)(2,1)}, u32[]{:S(2)}) copy-start(bf16[256,256]{1,0:T(8,128)(2,1)} %constant.17.clone.p2) | copy-start | bytes 393220
  2.9 1.0 %copy-start.2 = (bf16[256,384]{1,0:T(8,128)(2,1)S(1)}, bf16[256,384]{1,0:T(8,128)(2,1)}, u32[]{:S(2)}) copy-start(bf16[256,384]{1,0:T(8,128)(2,1)} %constant.15.clone.s2) | copy-start | bytes 589828
  2.9 1.0 %copy-start.3 = (bf16[128,768]{1,0:T(8,128)(2,1)S(1)}, bf16[128,768]{1,0:T(8,128)(2,1)}, u32[]{:S(2)}) copy-start(bf16[128,768]{1,0:T(8,128)(2,1)} %constant.16.clone.e1) | copy-start | bytes 589828
  2.9 1.0 %copy-start.4 = (bf16[256,192]{1,0:T(8,128)(2,1)S(1)}, bf16[256,192]{1,0:T(8,128)(2,1)}, u32[]{:S(2)}) copy-start(bf16[256,192]{1,0:T(8,128)(2,1)} %constant.14.clone.p1) | copy-start | bytes 294916
  3.1 1.0 %copy-start.1 = (bf16[256,384]{1,0:T(8,128)(2,1)S(1)}, bf16[256,384]{1,0:T(8,128)(2,1)}, u32[]{:S(2)}) copy-start(bf16[256,384]{1,0:T(8,128)(2,1)} %constant.13.clone.s1) | copy-start | bytes 589828
  3.1 1.0 %copy-start.6 = (f32[4]{0:T(128)S(1)}, f32[4]{0:T(128)}, u32[]{:S(2)}) copy-start(f32[4]{0:T(128)} %param.19) | copy-start | bytes 52
  3.1 1.0 %copy-start.7 = (f32[4]{0:T(128)S(1)}, f32[4]{0:T(128)}, u32[]{:S(2)}) copy-start(f32[4]{0:T(128)} %param.20) | copy-start | bytes 52

commit v2 on v1

v2 whole, which is shorter than its diff:
```python
import functools

import jax
import jax.numpy as jnp
import numpy as np
from jax import lax
from jax.experimental import pallas as pl
from jax.experimental.pallas import tpu as pltpu
from jax.sharding import PartitionSpec as P

MESH = pl.DeviceIdType.MESH
BF = jnp.bfloat16
F32 = jnp.float32
UNROLL = (1,) * 10


def depth_taps():
    z = np.arange(256)[:, None, None]
    k = np.arange(3)[None, :, None]
    p = np.arange(128)[None, None, :]
    return (z == 2 * p + k - 1).reshape(256, 384)


def rows_to_channels():
    out = np.zeros((16, 16, 12, 16), bool)
    for r in range(12):
        for y in range(16):
            out[y, r, r, y] = True
    return out.reshape(256, 192)


def depth_taps_low():
    out = np.zeros((2, 128, 3, 2, 64), bool)
    for h in range(2):
        for k in range(3):
            for p in range(64):
                if 2 * p + k - 1 >= 0:
                    out[h, 2 * p + k - 1, k, h, p] = True
    return out.reshape(256, 384)


def depth_spread():
    out = np.zeros((2, 64, 2, 3, 128), bool)
    for h in range(2):
        for k in range(3):
            for p in range(64):
                if 2 * p + k - 1 >= 0:
                    out[h, p, h, k, 2 * p + k - 1] = True
    return out.reshape(128, 768)


def channels_to_rows():
    out = np.zeros((16, 16, 16, 16), bool)
    for i in range(16):
        for y in range(16):
            out[i, y, y, i] = True
    return out.reshape(256, 256)


def low_order():
    out = np.zeros((512, 432), bool)
    for t in range(27):
        for i in range(16):
            out[t * 16 + i, i * 27 + t] = True
    return out


def high_order():
    out = np.zeros((2, 3, 5, 16, 128), bool)
    for s in range(2):
        for kx in range(3):
            for ky in range(3):
                for kz in range(3):
                    for c in range(4):
                        out[s, kx, ky + 2 * s, kz * 4 + c, c * 27 + kx * 9 + ky * 3 + kz] = True
    return out.reshape(2, 240, 128)


def mm(a, b):
    return lax.dot_general(a, b, (((1,), (0,)), ((), ())), preferred_element_type=F32)


def mm_nt(a, b):
    return lax.dot_general(a, b, (((1,), (1,)), ((), ())), preferred_element_type=F32)


def thirds(x):
    a = x.astype(BF)
    rest = x - a.astype(F32)
    b = rest.astype(BF)
    c = (rest - b.astype(F32)).astype(BF)
    return jnp.concatenate([a, b, c], axis=0)


def select(x, table):
    n = x.shape[0]
    out = mm(thirds(x), table)
    return out[0:n] + out[n:2 * n] + out[2 * n:3 * n]


def sigmoid(x):
    return jax.nn.sigmoid(x)


def kernel(
    nx, ny, cells,
    v, w1, b1, wl, bl, hw, hb, tg, wb, s1, p1, s2, e1, p2, ol, oh,
    bg_out, pred_out, head_out, low_out, low_bias, high_out,
    halo, a1, pre, act, taps, slope, slope_y, up, grad_b,
    pool_s, pool_1, pool_2, gsend, g_1, g_2s, g_2, g_3, h_s, h_1, h_2,
    hs, hr, ss, rs,
):
    sg = lax.axis_index("segment")
    mx = lax.axis_index("gx")
    my = lax.axis_index("gy")
    group = 2 * ny
    mg = sg * ny + my
    yu, yd = lax.rem(my + 1, ny), lax.rem(my + ny - 1, ny)
    xu = {"segment": 1 - sg, "gx": lax.rem(mx + sg, nx)}
    xd = {"segment": 1 - sg, "gx": lax.rem(mx + nx - 1 + sg, nx)}
    first_x = jnp.logical_and(mx == 0, sg == 0)
    last_x = jnp.logical_and(mx == nx - 1, sg == 1)

    def column(d):
        return {"gx": lax.rem(mx + d, nx)}

    def member(d):
        at = lax.rem(mg + d, group)
        return {"segment": at // ny, "gy": lax.rem(at, ny)}

    barrier = pltpu.get_barrier_semaphore()
    partners = [column(d) for d in range(1, nx)] + [member(d) for d in range(1, group)]
    partners += [xu, xd, {**xu, "gy": yu}, {**xd, "gy": yd}]
    for peer in partners:
        pl.semaphore_signal(barrier, inc=1, device_id=peer, device_id_type=MESH)

    copies = []

    def send(n, src, dst, peer):
        copy = pltpu.make_async_remote_copy(
            src_ref=src, dst_ref=dst, send_sem=hs.at[n], recv_sem=hr.at[n],
            device_id=peer, device_id_type=MESH,
        )
        copy.start()
        copies.append(copy)
        return copy

    stages = []

    def spread(stage, n, me, to, buffer, source):
        for d in range(1, n):
            pltpu.make_async_remote_copy(
                src_ref=source(lax.rem(me + d, n)), dst_ref=buffer.at[me],
                send_sem=ss.at[stage], recv_sem=rs.at[stage],
                device_id=to(d), device_id_type=MESH,
            ).start()
        stages.append((stage, buffer, n))

    def arrive(stage, buffer, n):
        ref = buffer.at[pl.ds(0, n - 1)]
        pltpu.make_async_copy(ref, ref, rs.at[stage]).wait()

    def add_up(buffer, n):
        part = buffer[0]
        for d in range(1, n):
            part = part + buffer[d]
        return part

    def to_channels(load, xs, yb):
        parts = []
        for h in range(2):
            raw = load(yb * 2 + h).reshape(64, 256)
            d = mm(raw, s1[...]).astype(BF)
            parts.append(jnp.concatenate([d[:, 0:128], d[:, 128:256], d[:, 256:384]], axis=0))
        out = mm(p1[...], jnp.concatenate(parts, axis=1)).astype(BF)
        for h in range(2):
            start = pl.multiple_of(16 + (yb * 2 + h) * 256, 16)
            a1[xs, pl.ds(start, 256), :] = out[:, h * 128:(h + 1) * 128]

    def own_plane(t, carry):
        x, yb = t // 2, lax.rem(t, 2)

        def load(b):
            return v[:, 4 * sg + x, pl.ds(pl.multiple_of(b * 16, 16), 16), :]

        to_channels(load, x + 1, yb)
        return carry

    lax.fori_loop(0, 8, own_plane, 0, unroll=UNROLL[0])
    pl.semaphore_wait(barrier, len(partners))

    c_raw = send(0, v.at[:, 4 * sg + 3], halo, xu)
    c_a1y = send(1, a1.at[pl.ds(1, 4), pl.ds(1024, 16)], a1.at[pl.ds(1, 4), pl.ds(0, 16)], {"gy": yu})
    c_a1c = send(2, a1.at[4, pl.ds(1024, 16)], a1.at[0, pl.ds(0, 16)], {**xu, "gy": yu})

    def conv_high(px, t):
        cols = []
        for h in range(2):
            start = pl.multiple_of(t * 128 + h * 64, 16)
            cols.append(jnp.concatenate([a1[2 * px + k, pl.ds(start, 80), :] for k in range(3)], axis=0))
        out = mm(w1[...], jnp.concatenate(cols, axis=1)) + b1[...]
        acts = (out * sigmoid(out)).astype(BF)
        for h in range(2):
            pre[px, pl.ds(pl.multiple_of(t * 64 + h * 32, 32), 32), :] = out[:, h * 128:(h + 1) * 128]
            start = pl.multiple_of(16 + t * 64 + h * 32, 16)
            act[px + 1, pl.ds(start, 32), :] = acts[:, h * 128:(h + 1) * 128]

    def conv_high_1(t, carry):
        conv_high(1, t)
        return carry

    def conv_high_0(t, carry):
        conv_high(0, t)
        return carry

    lax.fori_loop(1, 8, conv_high_1, 0, unroll=UNROLL[1])
    c_a1y.wait_recv()

    @pl.when(my == 0)
    def _():
        a1[1:5, 0:16, :] = jnp.zeros((4, 16, 128), BF)

    conv_high(1, 0)
    c_ax = send(3, act.at[2, pl.ds(16, 512)], act.at[0, pl.ds(16, 512)], xu)
    c_ac = send(4, act.at[2, pl.ds(512, 16)], act.at[0, pl.ds(0, 16)], {**xu, "gy": yu})
    c_raw.wait_recv()

    @pl.when(first_x)
    def _():
        halo[...] = jnp.zeros_like(halo)

    def halo_plane(yb, carry):
        def load(b):
            return halo[:, pl.ds(pl.multiple_of(b * 16, 16), 16), :]

        to_channels(load, 0, yb)
        return carry

    lax.fori_loop(0, 2, halo_plane, 0, unroll=UNROLL[2])
    c_a1c.wait_recv()

    @pl.when(jnp.logical_or(first_x, my == 0))
    def _():
        a1[0, 0:16, :] = jnp.zeros((16, 128), BF)

    conv_high(0, 7)
    c_ay = send(5, act.at[pl.ds(1, 2), pl.ds(512, 16)], act.at[pl.ds(1, 2), pl.ds(0, 16)], {"gy": yu})
    lax.fori_loop(0, 7, conv_high_0, 0, unroll=UNROLL[1])

    def to_taps(xs, first, count):
        low = act[xs, pl.ds(pl.multiple_of(16 * first, 16), 16 * count), :]
        high = act[xs, pl.ds(pl.multiple_of(256 + 16 * first, 16), 16 * count), :]
        d = mm(jnp.concatenate([low, high], axis=1), s2[...]).astype(BF)
        for t in range(count):
            for k in range(3):
                row = pl.multiple_of(((first + t) * 3 + k) * 16, 16)
                taps[xs, pl.ds(row, 16), :] = d[16 * t:16 * (t + 1), 128 * k:128 * (k + 1)]

    def taps_own(t, carry):
        to_taps(1 + t // 4, 1 + 4 * lax.rem(t, 4), 4)
        return carry

    def taps_halo(t, carry):
        to_taps(0, 1 + 4 * t, 4)
        return carry

    lax.fori_loop(0, 8, taps_own, 0, unroll=UNROLL[3])
    c_ay.wait_recv()
    c_ac.wait_recv()

    @pl.when(my == 0)
    def _():
        act[:, 0:16, :] = jnp.zeros((3, 16, 128), BF)

    to_taps(1, 0, 1)
    to_taps(2, 0, 1)
    c_ax.wait_recv()

    @pl.when(first_x)
    def _():
        act[0] = jnp.zeros((528, 128), BF)

    to_taps(0, 0, 1)
    lax.fori_loop(0, 4, taps_halo, 0, unroll=UNROLL[3])

    def window(j):
        start = pl.multiple_of(j * 96, 16)
        return jnp.concatenate([taps[k, pl.ds(start, 144), :] for k in range(3)], axis=0)

    def conv_low(t, total):
        out = mm(wl[...], jnp.concatenate([window(2 * t), window(2 * t + 1)], axis=1)) + bl[...]
        sig = sigmoid(out)
        slopes = (sig * (1.0 + out * (1.0 - sig))).astype(BF)
        values = out * sig
        for h in range(2):
            slope[0, pl.ds(pl.multiple_of(t * 64 + h * 32, 32), 32), :] = slopes[:, h * 128:(h + 1) * 128]
        return total + values[:, :128] + values[:, 128:]

    total = lax.fori_loop(0, 4, conv_low, jnp.zeros((32, 128), F32), unroll=UNROLL[4])

    lane = lax.broadcasted_iota(jnp.int32, (32, 128), 1)
    row = lax.broadcasted_iota(jnp.int32, (32, 128), 0)
    sums = jnp.sum(total, axis=1, keepdims=True)
    mine = jnp.broadcast_to(jnp.sum(jnp.where(lane == row, sums, 0.0), axis=0, keepdims=True), (8, 128))
    pool_s[0] = mine
    pool_1[mx] = mine
    spread(0, nx, mx, column, pool_1, lambda peer: pool_s.at[0])

    c_sx = send(6, slope.at[0], slope.at[1], xd)
    c_sy = send(7, slope.at[0, pl.ds(0, 32)], slope_y.at[0], {"gy": yd})
    c_sc = send(8, slope.at[0, pl.ds(0, 32)], slope_y.at[1], {**xd, "gy": yd})

    def low_back(t, carry):
        g, gb = carry
        us, ws = [], []
        for h in range(2):
            u = slope[0, pl.ds(pl.multiple_of(t * 64 + h * 32, 32), 32), :]
            us.append(u)
            ws.append(window(2 * t + h))
            gb = gb + u.astype(F32)
        g = g + mm_nt(jnp.concatenate(us, axis=1), jnp.concatenate(ws, axis=1))
        return g, gb

    g_low, gb_low = lax.fori_loop(
        0, 4, low_back, (jnp.zeros((32, 432), F32), jnp.zeros((32, 128), F32)), unroll=UNROLL[5]
    )
    last = jnp.concatenate(
        [g_low[:, 384:432], jnp.sum(gb_low, axis=1, keepdims=True), jnp.zeros((32, 79), F32)], axis=1
    )
    blocks = [g_low[:, 0:128], g_low[:, 128:256], g_low[:, 256:384], last]
    for b in range(4):
        for c in range(4):
            gsend[b * 4 + c] = blocks[c][8 * b:8 * (b + 1), :]
    per = 16 // nx
    g_1[mx] = gsend[pl.ds(mx * per, per)]
    spread(1, nx, mx, column, g_1, lambda peer: gsend.at[pl.ds(peer * per, per)])

    def spread_rows(px, t):
        u = slope[px, pl.ds(pl.multiple_of(t * 32, 32), 32), :]
        d = mm(u, e1[...]).astype(BF)
        for h in range(2):
            for k in range(3):
                start = pl.multiple_of(((8 * h + t) * 3 + k) * 32, 32)
                col = (h * 3 + k) * 128
                up[px, pl.ds(start, 32), :] = d[:, col:col + 128]

    def spread_own(t, carry):
        spread_rows(0, t)
        return carry

    def spread_halo(t, carry):
        spread_rows(1, t)
        return carry

    lax.fori_loop(0, 8, spread_own, 0, unroll=UNROLL[6])

    arrive(0, pool_1, nx)
    part = add_up(pool_1, nx)
    pool_s[1] = part
    pool_2[mg] = part
    spread(2, group, mg, member, pool_2, lambda peer: pool_s.at[1])

    c_sx.wait_recv()
    c_sy.wait_recv()
    c_sc.wait_recv()

    @pl.when(last_x)
    def _():
        slope[1] = jnp.zeros((256, 128), BF)
        slope_y[1] = jnp.zeros((32, 128), BF)

    @pl.when(my == ny - 1)
    def _():
        slope_y[...] = jnp.zeros((2, 32, 128), BF)

    lax.fori_loop(0, 8, spread_halo, 0, unroll=UNROLL[6])
    for px in range(2):
        d = mm(slope_y[px], e1[:, 0:384]).astype(BF)
        for k in range(3):
            up[px, (48 + k) * 32:(49 + k) * 32, :] = d[:, k * 128:(k + 1) * 128]

    def slope_high(t, carry):
        px, yp = t // 8, lax.rem(t, 8)
        at = pl.ds(pl.multiple_of(yp * 64, 64), 64)
        val = pre[px, at, :]
        sig = sigmoid(val)
        pre[px, at, :] = sig * (1.0 + val * (1.0 - sig))
        return carry

    lax.fori_loop(0, 16, slope_high, 0, unroll=UNROLL[7])

    arrive(1, g_1, nx)
    part = add_up(g_1, nx)
    g_2s[...] = part
    g_2[mg] = part
    spread(3, group, mg, member, g_2, lambda peer: g_2s)

    arrive(2, pool_2, group)
    part = add_up(pool_2, group)
    scale = 1.0 / cells
    pooled = jnp.sum(jnp.where(lane == row, part[0:1, :], 0.0), axis=1, keepdims=True) * scale
    weight = hw[...]
    predicted = jnp.sum(pooled * weight, axis=0, keepdims=True) + hb[...]
    error = predicted - tg[...]
    pred_out[...] = predicted
    head_out[...] = pooled * error
    signal = jnp.sum(weight * error, axis=1, keepdims=True)
    lanes = lax.rem(lax.broadcasted_iota(jnp.int32, (32, 384), 1), 32)
    rows = lax.broadcasted_iota(jnp.int32, (32, 384), 0)
    signal_row = jnp.sum(jnp.where(lanes == rows, signal, 0.0), axis=0, keepdims=True)
    weights = (wb[...].astype(F32) * signal_row).astype(BF)

    def high_back(t, carry):
        g, gb = carry
        cols = []
        for h in range(2):
            start = pl.multiple_of(t * 192 + h * 96, 32)
            cols.append(jnp.concatenate([up[0, pl.ds(start, 192), :], up[1, pl.ds(start, 192), :]], axis=0))
        out = mm(weights, jnp.concatenate(cols, axis=1)).astype(BF)
        ws, ups = [], []
        for h in range(2):
            at = pl.ds(pl.multiple_of(t * 64 + h * 32, 32), 32)
            begin = pl.multiple_of(t * 128 + h * 64, 16)
            for qx in range(2):
                tile = out[32 * qx:32 * (qx + 1), h * 128:(h + 1) * 128]
                grad_b[qx, at, :] = tile
                u = (tile.astype(F32) * pre[qx, at, :]).astype(BF)
                gb = gb + u.astype(F32)
                ups.append(u)
                ws.append(jnp.concatenate([a1[2 * qx + k, pl.ds(begin, 80), :] for k in range(3)], axis=0))
        g = g + mm_nt(jnp.concatenate(ups, axis=1), jnp.concatenate(ws, axis=1))
        return g, gb

    g_high, gb_high = lax.fori_loop(
        0, 8, high_back, (jnp.zeros((32, 240), F32), jnp.zeros((32, 128), F32)), unroll=UNROLL[8]
    )
    g_w = select(g_high[0:16], oh[0]) + select(g_high[16:32], oh[1])
    bias = jnp.sum(gb_high, axis=1, keepdims=True)
    lane16 = lax.broadcasted_iota(jnp.int32, (16, 128), 1)
    h_mine = jnp.where(lane16 == 108, bias[0:16] + bias[16:32], g_w) * scale
    h_s[0] = h_mine
    h_1[mx] = h_mine
    spread(4, nx, mx, column, h_1, lambda peer: h_s.at[0])

    arrive(3, g_2, group)
    part = add_up(g_2, group)
    g_3[mx] = part
    spread(5, nx, mx, column, g_3, lambda peer: g_3.at[mx])

    def place(t, carry):
        qx = t // 2
        h = lax.rem(t, 2)
        block = grad_b[qx, pl.ds(pl.multiple_of(h * 256, 256), 256), :]
        out = mm(p2[...], block).astype(BF).reshape(16, 16, 128)
        bg_out[:, 2 * sg + qx, pl.ds(pl.multiple_of(h * 16, 16), 16), :] = out
        return carry

    lax.fori_loop(0, 4, place, 0, unroll=UNROLL[9])
    half = bg_out.at[:, pl.ds(2 * sg, 2)]
    c_bg = send(9, half, half, {"segment": 1 - sg})

    arrive(4, h_1, nx)
    part = add_up(h_1, nx)
    h_s[1] = part
    h_2[mg] = part
    spread(6, group, mg, member, h_2, lambda peer: h_s.at[1])

    arrive(5, g_3, nx)
    bands = []
    for b in range(4):
        bands.append(jnp.concatenate([g_3[(b * 4 + c) // per, (b * 4 + c) % per] for c in range(4)], axis=1))
    g_all = jnp.concatenate(bands, axis=0) * (signal * scale)
    low_out[...] = select(g_all, ol[...])
    low_bias[...] = g_all[:, 432:433]

    arrive(6, h_2, group)
    high_out[...] = add_up(h_2, group)
    c_bg.wait_recv()
    for copy in copies:
        copy.wait_send()
    for stage, buffer, n in stages:
        ref = buffer.at[pl.ds(0, n - 1)]
        pltpu.make_async_copy(ref, ref, ss.at[stage]).wait()


def shards(nx, ny, volume, weight_high, bias_high, weight_low, bias_low, head_weight, head_bias, targets):
    cells = 2 * nx * 16 * ny * 64
    wh = jnp.transpose(weight_high, (0, 2, 3, 4, 1))
    wh = jnp.pad(wh, ((0, 0), (0, 0), (0, 0), (0, 1), (0, 0))).reshape(16, 3, 3, 16)
    w1 = jnp.concatenate(
        [
            jnp.pad(wh, ((0, 0), (0, 0), (0, 2), (0, 0))).reshape(16, 240),
            jnp.pad(wh, ((0, 0), (0, 0), (2, 0), (0, 0))).reshape(16, 240),
        ],
        axis=0,
    )
    wl = jnp.transpose(weight_low, (0, 2, 3, 4, 1)).reshape(32, 432)
    wt = jnp.transpose(weight_low, (1, 2, 3, 4, 0))
    wt = jnp.pad(wt, ((0, 0), (0, 1), (0, 1), (0, 0), (0, 0)))
    tap = ((1, 3), (2, 0))
    wb = jnp.stack(
        [
            jnp.stack([wt[:, tap[sx][dx], tap[sy][dy]] for dx in range(2) for dy in range(2)], axis=1)
            for sx in range(2)
            for sy in range(2)
        ],
        axis=0,
    ).reshape(64, 384)
    b1 = jnp.concatenate([bias_high, bias_high])[:, None]
    makers = (depth_taps, rows_to_channels, depth_taps_low, depth_spread, channels_to_rows, low_order, high_order)
    tables = [jnp.asarray(t().astype(np.float32), BF) for t in makers]
    vm = pl.BlockSpec(memory_space=pltpu.VMEM)
    dma = pltpu.SemaphoreType.DMA
    per = 16 // nx
    group = 2 * ny
    bg, pred, head, low, low_bias, high = pl.pallas_call(
        functools.partial(kernel, nx, ny, cells),
        out_shape=(
            jax.ShapeDtypeStruct((16, 4, 32, 128), BF),
            jax.ShapeDtypeStruct((1, 4), F32),
            jax.ShapeDtypeStruct((32, 4), F32),
            jax.ShapeDtypeStruct((32, 432), F32),
            jax.ShapeDtypeStruct((32, 1), F32),
            jax.ShapeDtypeStruct((16, 128), F32),
        ),
        in_specs=[vm] * 16,
        out_specs=(vm,) * 6,
        scratch_shapes=[
            pltpu.VMEM((4, 64, 256), BF),
            pltpu.VMEM((5, 1040, 128), BF),
            pltpu.VMEM((2, 512, 128), F32),
            pltpu.VMEM((3, 528, 128), BF),
            pltpu.VMEM((3, 816, 128), BF),
            pltpu.VMEM((2, 256, 128), BF),
            pltpu.VMEM((2, 32, 128), BF),
            pltpu.VMEM((2, 1632, 128), BF),
            pltpu.VMEM((2, 512, 128), BF),
            pltpu.VMEM((2, 8, 128), F32),
            pltpu.VMEM((nx, 8, 128), F32),
            pltpu.VMEM((group, 8, 128), F32),
            pltpu.VMEM((16, 8, 128), F32),
            pltpu.VMEM((nx, per, 8, 128), F32),
            pltpu.VMEM((per, 8, 128), F32),
            pltpu.VMEM((group, per, 8, 128), F32),
            pltpu.VMEM((nx, per, 8, 128), F32),
            pltpu.VMEM((2, 16, 128), F32),
            pltpu.VMEM((nx, 16, 128), F32),
            pltpu.VMEM((group, 16, 128), F32),
            dma((10,)), dma((10,)), dma((7,)), dma((7,)),
        ],
        compiler_params=pltpu.CompilerParams(
            collective_id=0, has_side_effects=True, vmem_limit_bytes=48 << 20
        ),
        name="fused",
    )(
        volume, w1, b1, wl, bias_low[:, None], head_weight, head_bias[None], targets[None], wb, *tables
    )
    return (
        pred[0],
        bg,
        high[:, :108].reshape(16, 4, 3, 3, 3),
        high[:, 108],
        low.reshape(32, 16, 3, 3, 3),
        low_bias[:, 0],
        head,
    )


def solution(mesh):
    nx, ny = mesh.shape["gx"], mesh.shape["gy"]
    placed = (P(None, "gx", "gy", None), P(), P(), P(), P(), P(), P(), P())
    return jax.shard_map(
        functools.partial(shards, nx, ny),
        mesh=mesh,
        in_specs=placed,
        out_specs=(P(), P(None, "gx", "gy", None), P(), P(), P(), P(), P()),
        check_vma=False,
    )
```

time: 79.6 us -> 56.3 us (0.71)
  the two profiles are of different devices: /device:TPU:8 before, /device:TPU:1 now
where the time goes in v2:
time: 56.3 us; the launch traced here: 56.1 us
  Pallas kernels  45.3 us (80%)
  local copies, waits for them, and re-layouts  9.1 us (16%)
  between operations  0.88 us (2%)
  other arithmetic  0.81 us (1%)
    pallas_call x1, Pallas kernels, shards(): pl.pallas_call(functools.partial(kernel, nx, ny, cells), out_shape=(jax.S...  45.3 us
    unnamed x32, local copies, waits for them, and re-layouts  4.56 us

profile of v2, /device:TPU:1, one launch (start us, length us, event | category | flops | bytes accessed | tf_op | source)
XLA Modules:
  0.0 56.1 jit_solution(5696250895904140688)
XLA Ops:
  0.6 0.0 copy-start.7
  0.6 0.8 %pad.14 = bf16[16,3,3,4,4]{0,4,3,2,1:T(4,128)(2,1)S(1)} pad(bf16[16,3,3,3,4]{0,4,3,2,1:T(4,128)(2,1)} %bitcast.50, bf16[]{:T(256)} %constant.16.clone.1), padding=0_0x0_0x0_0x0_1x0_0 | pad | bytes 8066 | tf_op jit(solution)/shard_map/jit(_pad)/pad | solution.py:489
  1.5 0.1 copy.32
  1.6 0.0 copy-start.5
  1.6 0.0 copy-start.6
  1.6 0.1 fusion.4
  1.7 0.0 copy-start.12
  1.7 0.0 copy-start.11
  1.7 0.0 copy-start.10
  1.7 0.0 copy-start.4
  1.7 0.1 reshape.37
  1.8 0.0 copy-start
  1.8 0.1 reshape.36
  2.0 0.4 copy-done.12
  2.3 0.1 maximum_bitcast_fusion.1
  2.4 0.1 copy.35.b1
  2.5 1.0 %copy.36.wl = bf16[32,432]{1,0:T(8,128)(2,1)S(1)} copy(bf16[32,432]{0,1:T(8,128)(2,1)} %bitcast.47) | data formatting | bytes 55296 | tf_op jit(solution)/shard_map/reshape | solution.py:497
  3.5 0.0 copy-done.11
  3.5 0.1 copy.37.bl
  3.6 0.0 copy-done.10
  3.6 0.1 copy.38.hw
  3.7 0.9 %slice_bitcast_fusion.8 = (bf16[16,1,3,32]{3,0,2,1:T(8,128)(2,1)S(1)}, bf16[16,1,3,32]{3,0,2,1:T(8,128)(2,1)S(1)}, bf16[16,1,3,32]{3,0,2,1:T(8,128)(2,1)S(1)}, b...) fusion(bf16[16,3,3,3,32]{4,0,3,2,1:T(8,128)(2,1)} %bitcast.48), kind=kLoop, calls=%fused_computation.22 | loop fusion | bytes 55296 | tf_op jit(solution)/shard_map/stack;squeeze | solution.py:503
  4.6 0.0 copy-start.1
  4.6 0.1 pad_maximum_fusion
  4.7 0.0 copy-start.3
  4.7 0.1 copy.34
  4.8 0.0 copy-start.2
  4.8 0.0 copy-start.8
  4.8 0.0 copy-start.9
  4.8 0.2 reshape.39.wb
  5.0 0.0 copy-done.7
  5.0 0.0 copy-done.5
  5.0 0.0 copy-done.6
  5.1 0.0 copy-done.4
  5.1 0.0 copy-done
  5.1 0.6 %copy-done.1 = bf16[512,432]{1,0:T(8,128)(2,1)S(1)} copy-done((bf16[512,432]{1,0:T(8,128)(2,1)S(1)}, bf16[512,432]{1,0:T(8,128)(2,1)}, u32[]{:S(2)}) %copy-start.1) | copy-done | bytes 442392
  5.6 0.1 copy-done.3
  5.7 0.1 copy-done.2
  5.8 0.0 copy-done.8
  5.8 0.0 copy-done.9
  5.8 45.3 %fused.1 = (bf16[16,4,32,128]{3,2,1,0:T(8,128)(2,1)S(1)}, f32[1,4]{1,0:T(1,128)S(1)}, f32[32,4]{1,0:T(8,128)S(1)}, f32[32,432]{1,0:T(8,128)S(1)}, f32[32,1]{1,0:T(8,128)S(1)}, /*index=5*/f32[16,128]{1,0:T(8,128)S(1)}) custom-call(bf16[4,8,64,256]{3,2,1,0:T(8,128)(2,1)S(1)} %copy-done, bf16[32,240]{1,0:T(8,128)(2,1)S(1)} %pad_maximum_fusion.8.w1, ...), custom_call_target="tpu_custom_call" | custom-call | tf_op jit(solution)/shard_map/fused/pallas_call | solution.py:516
  51.1 0.1 copy.39
  51.3 0.6 %copy.41 = f32[16,4,3,3,3]{0,1,4,3,2:T(4,128)} copy(f32[16,4,3,3,3]{0,4,3,2,1:T(4,128)S(1)} %reshape.40) | data formatting | bytes 13824
  51.9 0.7 %slice_reduce_fusion = f32[16]{0:T(128)} fusion(f32[16,128]{1,0:T(8,128)S(1)} %get-tuple-element.15), kind=kLoop, calls=%fused_computation.23 | loop fusion | bytes 128 | tf_op jit(solution)/shard_map/slice | solution.py:562
  52.6 0.1 copy.40
  52.7 0.1 reshape.41
  52.8 0.7 %copy.42 = f32[32,16,3,3,3]{0,1,4,3,2:T(8,128)} copy(f32[32,16,3,3,3]{0,4,3,2,1:T(4,128)S(1)} %reshape.41) | data formatting | bytes 110592
  53.5 0.6 %reduce.1 = f32[32]{0:T(128)} reduce(f32[32,1]{1,0:T(8,128)S(1)} %get-tuple-element.17, f32[]{:T(128)} %constant.31), dimensions={1}, to_apply=%get-tuple-element.17.reduce_sub_computation | reduce | bytes 260 | tf_op jit(solution)/shard_map/fused/pallas_call | solution.py:516
  54.2 0.7 %copy.43 = f32[32,4]{0,1:T(4,128)} copy(f32[32,4]{1,0:T(8,128)S(1)} %get-tuple-element.32) | data formatting | bytes 1024
  54.8 0.5 copy.46
  55.3 0.8 %copy.47 = bf16[16,4,32,128]{3,2,1,0:T(8,128)(2,1)} copy(bf16[16,4,32,128]{3,2,1,0:T(8,128)(2,1)S(1)} %get-tuple-element.56) | data formatting | bytes 1048576
  (4 shorter events, 0.1 us)
Async XLA Ops:
  0.6 4.4 %copy-start.7 = (bf16[2,240,128]{2,1,0:T(8,128)(2,1)S(1)}, bf16[2,240,128]{2,1,0:T(8,128)(2,1)}, u32[]{:S(2)}) copy-start(bf16[2,240,128]{2,1,0:T(8,128)(2,1)} %constant.23.clone.oh) | copy-start | bytes 368644
  1.6 3.5 %copy-start.5 = (bf16[256,192]{1,0:T(8,128)(2,1)S(1)}, bf16[256,192]{1,0:T(8,128)(2,1)}, u32[]{:S(2)}) copy-start(bf16[256,192]{1,0:T(8,128)(2,1)} %constant.18.clone.p1) | copy-start | bytes 294916
  1.6 3.5 %copy-start.6 = (bf16[256,256]{1,0:T(8,128)(2,1)S(1)}, bf16[256,256]{1,0:T(8,128)(2,1)}, u32[]{:S(2)}) copy-start(bf16[256,256]{1,0:T(8,128)(2,1)} %constant.21.clone.p2) | copy-start | bytes 393220
  1.7 0.7 %copy-start.12 = (f32[16]{0:T(128)S(1)}, f32[16]{0:T(128)}, u32[]{:S(2)}) copy-start(f32[16]{0:T(128)} %param.17) | copy-start | bytes 196
  1.7 1.8 %copy-start.11 = (f32[32]{0:T(128)S(1)}, f32[32]{0:T(128)}, u32[]{:S(2)}) copy-start(f32[32]{0:T(128)} %param.19) | copy-start | bytes 388
  1.7 1.9 %copy-start.10 = (f32[32,4]{0,1:T(4,128)S(1)}, f32[32,4]{0,1:T(4,128)}, u32[]{:S(2)}) copy-start(f32[32,4]{0,1:T(4,128)} %param.20) | copy-start | bytes 1540
  1.7 3.4 %copy-start.4 = (bf16[128,768]{1,0:T(8,128)(2,1)S(1)}, bf16[128,768]{1,0:T(8,128)(2,1)}, u32[]{:S(2)}) copy-start(bf16[128,768]{1,0:T(8,128)(2,1)} %constant.20.clone.e1) | copy-start | bytes 589828
  1.8 3.3 %copy-start = (bf16[4,8,64,256]{3,2,1,0:T(8,128)(2,1)S(1)}, bf16[4,8,64,256]{3,2,1,0:T(8,128)(2,1)}, u32[]{:S(2)}) copy-start(bf16[4,8,64,256]{3,2,1,0:T(8,128)(2,1)} %v.1) | copy-start | bytes 3145732
  4.6 1.0 %copy-start.1 = (bf16[512,432]{1,0:T(8,128)(2,1)S(1)}, bf16[512,432]{1,0:T(8,128)(2,1)}, u32[]{:S(2)}) copy-start(bf16[512,432]{1,0:T(8,128)(2,1)} %constant.22.clone.ol) | copy-start | bytes 1327108
  4.7 1.0 %copy-start.3 = (bf16[256,384]{1,0:T(8,128)(2,1)S(1)}, bf16[256,384]{1,0:T(8,128)(2,1)}, u32[]{:S(2)}) copy-start(bf16[256,384]{1,0:T(8,128)(2,1)} %constant.19.clone.s2) | copy-start | bytes 589828
  4.8 1.0 %copy-start.2 = (bf16[256,384]{1,0:T(8,128)(2,1)S(1)}, bf16[256,384]{1,0:T(8,128)(2,1)}, u32[]{:S(2)}) copy-start(bf16[256,384]{1,0:T(8,128)(2,1)} %constant.17.clone.s1) | copy-start | bytes 589828
  4.8 1.0 %copy-start.8 = (f32[4]{0:T(128)S(1)}, f32[4]{0:T(128)}, u32[]{:S(2)}) copy-start(f32[4]{0:T(128)} %param.21) | copy-start | bytes 52
  4.8 1.0 %copy-start.9 = (f32[4]{0:T(128)S(1)}, f32[4]{0:T(128)}, u32[]{:S(2)}) copy-start(f32[4]{0:T(128)} %param.22) | copy-start | bytes 52

commit v3 on v2

--- a/solution.py
+++ b/solution.py
@@ -11,7 +11,7 @@
 MESH = pl.DeviceIdType.MESH
 BF = jnp.bfloat16
 F32 = jnp.float32
-UNROLL = (1,) * 10
+UNROLL = (8, 4, 2, 4, 4, 4, 4, 4, 8, 4)
 
 
 def depth_taps():
@@ -57,14 +57,6 @@
     return out.reshape(256, 256)
 
 
-def low_order():
-    out = np.zeros((512, 432), bool)
-    for t in range(27):
-        for i in range(16):
-            out[t * 16 + i, i * 27 + t] = True
-    return out
-
-
 def high_order():
     out = np.zeros((2, 3, 5, 16, 128), bool)
     for s in range(2):
@@ -72,8 +64,26 @@
             for ky in range(3):
                 for kz in range(3):
                     for c in range(4):
-                        out[s, kx, ky + 2 * s, kz * 4 + c, c * 27 + kx * 9 + ky * 3 + kz] = True
+                        out[s, kx, ky + 2 * s, kz * 4 + c, ((kx * 3 + ky) * 3 + kz) * 4 + c] = True
     return out.reshape(2, 240, 128)
+
+
+def early_tables():
+    out = np.zeros((256, 896), np.float32)
+    out[:, 0:384] = depth_taps()
+    out[:, 384:576] = rows_to_channels()
+    out[0:240, 640:768], out[0:240, 768:896] = high_order()
+    return out
+
+
+def late_tables():
+    out = np.zeros((256, 1024), np.float32)
+    out[:, 0:384] = depth_taps_low()
+    out[:, 384:640] = channels_to_rows()
+    spread = depth_spread()
+    out[0:128, 640:1024] = spread[:, 0:384]
+    out[128:256, 640:1024] = spread[:, 384:768]
+    return out
 
 
 def mm(a, b):
@@ -104,12 +114,17 @@
 
 def kernel(
     nx, ny, cells,
-    v, w1, b1, wl, bl, hw, hb, tg, wb, s1, p1, s2, e1, p2, ol, oh,
-    bg_out, pred_out, head_out, low_out, low_bias, high_out,
-    halo, a1, pre, act, taps, slope, slope_y, up, grad_b,
-    pool_s, pool_1, pool_2, gsend, g_1, g_2s, g_2, g_3, h_s, h_1, h_2,
-    hs, hr, ss, rs,
+    v_hbm, ta_hbm, tb_hbm, *rest,
 ):
+    small_hbm, rest = rest[:7], rest[7:]
+    (
+        bg_out, pred_out, head_out, low_out, low_bias, high_out, high_bias,
+        v, ta, tb, wh, wlt, bh_row, bl_row, hw, hb_row, tg_row,
+        w_tall, wl, wb, h_tall, ls,
+        halo, a1, pre, act, taps, slope, slope_y, up, grad_b,
+        pool_s, pool_1, pool_2, gsend, g_1, g_2s, g_2, g_3, h_s, h_1, h_2,
+        hs, hr, ss, rs,
+    ) = rest
     sg = lax.axis_index("segment")
     mx = lax.axis_index("gx")
     my = lax.axis_index("gy")
@@ -121,15 +136,36 @@
     first_x = jnp.logical_and(mx == 0, sg == 0)
     last_x = jnp.logical_and(mx == nx - 1, sg == 1)
 
-    def column(d):
-        return {"gx": lax.rem(mx + d, nx)}
-
-    def member(d):
-        at = lax.rem(mg + d, group)
-        return {"segment": at // ny, "gy": lax.rem(at, ny)}
+    loads = [
+        pltpu.make_async_copy(v_hbm.at[:, pl.ds(4 * sg, 4)], v, ls.at[0]),
+        pltpu.make_async_copy(ta_hbm, ta, ls.at[1]),
+    ]
+    for n, (src, dst) in enumerate(zip(small_hbm, (wh, wlt, bh_row, bl_row, hw, hb_row, tg_row))):
+        loads.append(pltpu.make_async_copy(src, dst, ls.at[2 + n]))
+    loads.append(pltpu.make_async_copy(tb_hbm, tb, ls.at[9]))
+    for load in loads:
+        load.start()
+
+    columns, members = [], []
+    if nx == 16:
+        far = [(a, b) for a in range(4) for b in range(4) if a or b]
+        far.sort(key=lambda t: -min(t[0], 4 - t[0]) - min(t[1], 4 - t[1]))
+        for a, b in far:
+            at = lax.rem(mx // 4 + a, 4) * 4 + lax.rem(lax.rem(mx, 4) + b, 4)
+            columns.append((at, {"gx": at}))
+    else:
+        for d in range(1, nx):
+            at = lax.rem(mx + d, nx)
+            columns.append((at, {"gx": at}))
+    far = [(a, b) for a in range(2) for b in range(ny) if a or b]
+    far.sort(key=lambda t: -min(t[1], ny - t[1]))
+    for a, b in far:
+        seg = 1 - sg if a else sg
+        at = lax.rem(my + b, ny)
+        members.append((seg * ny + at, {"segment": seg, "gy": at}))
 
     barrier = pltpu.get_barrier_semaphore()
-    partners = [column(d) for d in range(1, nx)] + [member(d) for d in range(1, group)]
+    partners = [peer for _, peer in columns + members]
     partners += [xu, xd, {**xu, "gy": yu}, {**xd, "gy": yd}]
     for peer in partners:
         pl.semaphore_signal(barrier, inc=1, device_id=peer, device_id_type=MESH)
@@ -147,14 +183,14 @@
 
     stages = []
 
-    def spread(stage, n, me, to, buffer, source):
-        for d in range(1, n):
+    def spread(stage, me, peers, buffer, source):
+        for at, peer in peers:
             pltpu.make_async_remote_copy(
-                src_ref=source(lax.rem(me + d, n)), dst_ref=buffer.at[me],
+                src_ref=source(at), dst_ref=buffer.at[me],
                 send_sem=ss.at[stage], recv_sem=rs.at[stage],
-                device_id=to(d), device_id_type=MESH,
+                device_id=peer, device_id_type=MESH,
             ).start()
-        stages.append((stage, buffer, n))
+        stages.append((stage, buffer, len(peers) + 1))
 
     def arrive(stage, buffer, n):
         ref = buffer.at[pl.ds(0, n - 1)]
@@ -170,9 +206,9 @@
         parts = []
         for h in range(2):
             raw = load(yb * 2 + h).reshape(64, 256)
-            d = mm(raw, s1[...]).astype(BF)
+            d = mm(raw, ta[:, 0:384]).astype(BF)
             parts.append(jnp.concatenate([d[:, 0:128], d[:, 128:256], d[:, 256:384]], axis=0))
-        out = mm(p1[...], jnp.concatenate(parts, axis=1)).astype(BF)
+        out = mm(ta[:, 384:576], jnp.concatenate(parts, axis=1)).astype(BF)
         for h in range(2):
             start = pl.multiple_of(16 + (yb * 2 + h) * 256, 16)
             a1[xs, pl.ds(start, 256), :] = out[:, h * 128:(h + 1) * 128]
@@ -181,15 +217,41 @@
         x, yb = t // 2, lax.rem(t, 2)
 
         def load(b):
-            return v[:, 4 * sg + x, pl.ds(pl.multiple_of(b * 16, 16), 16), :]
+            return v[:, x, pl.ds(pl.multiple_of(b * 16, 16), 16), :]
 
         to_channels(load, x + 1, yb)
         return carry
 
+    loads[0].wait()
+    loads[1].wait()
     lax.fori_loop(0, 8, own_plane, 0, unroll=UNROLL[0])
+
+    for load in loads[2:]:
+        load.wait()
+
+    def eye(n):
+        r = lax.broadcasted_iota(jnp.int32, (n, n), 0)
+        return r == lax.broadcasted_iota(jnp.int32, (n, n), 1)
+
+    def to_column(row):
+        n = row.shape[1]
+        return jnp.sum(jnp.where(eye(n), row, 0.0), axis=1, keepdims=True)
+
+    w_tall[...] = jnp.zeros_like(w_tall)
+    for t in range(27):
+        w_tall[4 * t:4 * t + 4, :] = wh[t].astype(F32)
+    w_flat = mm_nt(eye(16).astype(F32).astype(BF), w_tall[...].astype(BF)).astype(BF)
+    w1 = jnp.concatenate(
+        [mm_nt(w_flat, ta[0:240, 640:768]), mm_nt(w_flat, ta[0:240, 768:896])], axis=0
+    ).astype(BF)
+    wl[...] = mm_nt(eye(32).astype(F32).astype(BF), wlt[...]).astype(BF)
+    b1 = to_column(bh_row[...])
+    b1 = jnp.concatenate([b1, b1], axis=0)
+    bl = to_column(bl_row[...])
+
     pl.semaphore_wait(barrier, len(partners))
 
-    c_raw = send(0, v.at[:, 4 * sg + 3], halo, xu)
+    c_raw = send(0, v.at[:, 3], halo, xu)
     c_a1y = send(1, a1.at[pl.ds(1, 4), pl.ds(1024, 16)], a1.at[pl.ds(1, 4), pl.ds(0, 16)], {"gy": yu})
     c_a1c = send(2, a1.at[4, pl.ds(1024, 16)], a1.at[0, pl.ds(0, 16)], {**xu, "gy": yu})
 
@@ -198,7 +260,7 @@
         for h in range(2):
             start = pl.multiple_of(t * 128 + h * 64, 16)
             cols.append(jnp.concatenate([a1[2 * px + k, pl.ds(start, 80), :] for k in range(3)], axis=0))
-        out = mm(w1[...], jnp.concatenate(cols, axis=1)) + b1[...]
+        out = mm(w1, jnp.concatenate(cols, axis=1)) + b1
         acts = (out * sigmoid(out)).astype(BF)
         for h in range(2):
             pre[px, pl.ds(pl.multiple_of(t * 64 + h * 32, 32), 32), :] = out[:, h * 128:(h + 1) * 128]
@@ -250,7 +312,7 @@
     def to_taps(xs, first, count):
         low = act[xs, pl.ds(pl.multiple_of(16 * first, 16), 16 * count), :]
         high = act[xs, pl.ds(pl.multiple_of(256 + 16 * first, 16), 16 * count), :]
-        d = mm(jnp.concatenate([low, high], axis=1), s2[...]).astype(BF)
+        d = mm(jnp.concatenate([low, high], axis=1), tb[:, 0:384]).astype(BF)
         for t in range(count):
             for k in range(3):
                 row = pl.multiple_of(((first + t) * 3 + k) * 16, 16)
@@ -288,7 +350,7 @@
         return jnp.concatenate([taps[k, pl.ds(start, 144), :] for k in range(3)], axis=0)
 
     def conv_low(t, total):
-        out = mm(wl[...], jnp.concatenate([window(2 * t), window(2 * t + 1)], axis=1)) + bl[...]
+        out = mm(wl[...], jnp.concatenate([window(2 * t), window(2 * t + 1)], axis=1)) + bl
         sig = sigmoid(out)
         slopes = (sig * (1.0 + out * (1.0 - sig))).astype(BF)
         values = out * sig
@@ -304,7 +366,7 @@
     mine = jnp.broadcast_to(jnp.sum(jnp.where(lane == row, sums, 0.0), axis=0, keepdims=True), (8, 128))
     pool_s[0] = mine
     pool_1[mx] = mine
-    spread(0, nx, mx, column, pool_1, lambda peer: pool_s.at[0])
+    spread(0, mx, columns, pool_1, lambda peer: pool_s.at[0])
 
     c_sx = send(6, slope.at[0], slope.at[1], xd)
     c_sy = send(7, slope.at[0, pl.ds(0, 32)], slope_y.at[0], {"gy": yd})
@@ -333,16 +395,15 @@
             gsend[b * 4 + c] = blocks[c][8 * b:8 * (b + 1), :]
     per = 16 // nx
     g_1[mx] = gsend[pl.ds(mx * per, per)]
-    spread(1, nx, mx, column, g_1, lambda peer: gsend.at[pl.ds(peer * per, per)])
+    spread(1, mx, columns, g_1, lambda peer: gsend.at[pl.ds(peer * per, per)])
 
     def spread_rows(px, t):
         u = slope[px, pl.ds(pl.multiple_of(t * 32, 32), 32), :]
-        d = mm(u, e1[...]).astype(BF)
-        for h in range(2):
+        for h in range(2):
+            d = mm(u, tb[128 * h:128 * (h + 1), 640:1024]).astype(BF)
             for k in range(3):
                 start = pl.multiple_of(((8 * h + t) * 3 + k) * 32, 32)
-                col = (h * 3 + k) * 128
-                up[px, pl.ds(start, 32), :] = d[:, col:col + 128]
+                up[px, pl.ds(start, 32), :] = d[:, k * 128:(k + 1) * 128]
 
     def spread_own(t, carry):
         spread_rows(0, t)
@@ -358,7 +419,7 @@
     part = add_up(pool_1, nx)
     pool_s[1] = part
     pool_2[mg] = part
-    spread(2, group, mg, member, pool_2, lambda peer: pool_s.at[1])
+    spread(2, mg, members, pool_2, lambda peer: pool_s.at[1])
 
     c_sx.wait_recv()
     c_sy.wait_recv()
@@ -375,7 +436,7 @@
 
     lax.fori_loop(0, 8, spread_halo, 0, unroll=UNROLL[6])
     for px in range(2):
-        d = mm(slope_y[px], e1[:, 0:384]).astype(BF)
+        d = mm(slope_y[px], tb[0:128, 640:1024]).astype(BF)
         for k in range(3):
             up[px, (48 + k) * 32:(49 + k) * 32, :] = d[:, k * 128:(k + 1) * 128]
 
@@ -389,26 +450,30 @@
 
     lax.fori_loop(0, 16, slope_high, 0, unroll=UNROLL[7])
 
+    wb[...] = jnp.zeros_like(wb)
+    for kx in range(3):
+        for ky in range(3):
+            for kz in range(3):
+                r = (2 * (kx != 1) + (ky != 1)) * 16
+                c = (2 * (kx == 0) + (ky == 0)) * 96 + kz * 32
+                t = ((kx * 3 + ky) * 3 + kz) * 16
+                wb[r:r + 16, c:c + 32] = wlt[t:t + 16, :]
+
     arrive(1, g_1, nx)
     part = add_up(g_1, nx)
     g_2s[...] = part
     g_2[mg] = part
-    spread(3, group, mg, member, g_2, lambda peer: g_2s)
+    spread(3, mg, members, g_2, lambda peer: g_2s)
 
     arrive(2, pool_2, group)
     part = add_up(pool_2, group)
     scale = 1.0 / cells
-    pooled = jnp.sum(jnp.where(lane == row, part[0:1, :], 0.0), axis=1, keepdims=True) * scale
+    pooled = part[0:1, 0:32] * scale
     weight = hw[...]
-    predicted = jnp.sum(pooled * weight, axis=0, keepdims=True) + hb[...]
-    error = predicted - tg[...]
-    pred_out[...] = predicted
-    head_out[...] = pooled * error
-    signal = jnp.sum(weight * error, axis=1, keepdims=True)
-    lanes = lax.rem(lax.broadcasted_iota(jnp.int32, (32, 384), 1), 32)
-    rows = lax.broadcasted_iota(jnp.int32, (32, 384), 0)
-    signal_row = jnp.sum(jnp.where(lanes == rows, signal, 0.0), axis=0, keepdims=True)
-    weights = (wb[...].astype(F32) * signal_row).astype(BF)
+    predicted = jnp.sum(weight * pooled, axis=1, keepdims=True) + to_column(hb_row[...])
+    error = predicted - to_column(tg_row[...])
+    signal = jnp.sum(weight * error, axis=0, keepdims=True)
+    weights = (wb[...].astype(F32) * jnp.concatenate([signal] * 12, axis=1)).astype(BF)
 
     def high_back(t, carry):
         g, gb = carry
@@ -434,24 +499,24 @@
     g_high, gb_high = lax.fori_loop(
         0, 8, high_back, (jnp.zeros((32, 240), F32), jnp.zeros((32, 128), F32)), unroll=UNROLL[8]
     )
-    g_w = select(g_high[0:16], oh[0]) + select(g_high[16:32], oh[1])
+    g_w = select(g_high[0:16], ta[0:240, 640:768]) + select(g_high[16:32], ta[0:240, 768:896])
     bias = jnp.sum(gb_high, axis=1, keepdims=True)
     lane16 = lax.broadcasted_iota(jnp.int32, (16, 128), 1)
     h_mine = jnp.where(lane16 == 108, bias[0:16] + bias[16:32], g_w) * scale
     h_s[0] = h_mine
     h_1[mx] = h_mine
-    spread(4, nx, mx, column, h_1, lambda peer: h_s.at[0])
+    spread(4, mx, columns, h_1, lambda peer: h_s.at[0])
 
     arrive(3, g_2, group)
     part = add_up(g_2, group)
     g_3[mx] = part
-    spread(5, nx, mx, column, g_3, lambda peer: g_3.at[mx])
+    spread(5, mx, columns, g_3, lambda peer: g_3.at[mx])
 
     def place(t, carry):
         qx = t // 2
         h = lax.rem(t, 2)
         block = grad_b[qx, pl.ds(pl.multiple_of(h * 256, 256), 256), :]
-        out = mm(p2[...], block).astype(BF).reshape(16, 16, 128)
+        out = mm(tb[:, 384:640], block).astype(BF).reshape(16, 16, 128)
         bg_out[:, 2 * sg + qx, pl.ds(pl.multiple_of(h * 16, 16), 16), :] = out
         return carry
 
@@ -463,18 +528,23 @@
     part = add_up(h_1, nx)
     h_s[1] = part
     h_2[mg] = part
-    spread(6, group, mg, member, h_2, lambda peer: h_s.at[1])
+    spread(6, mg, members, h_2, lambda peer: h_s.at[1])
 
     arrive(5, g_3, nx)
     bands = []
     for b in range(4):
         bands.append(jnp.concatenate([g_3[(b * 4 + c) // per, (b * 4 + c) % per] for c in range(4)], axis=1))
-    g_all = jnp.concatenate(bands, axis=0) * (signal * scale)
-    low_out[...] = select(g_all, ol[...])
-    low_bias[...] = g_all[:, 432:433]
+    g_all = jnp.transpose(jnp.concatenate(bands, axis=0)) * (signal * scale)
+    low_out[...] = g_all[0:432, :]
+    low_bias[...] = g_all[432:433, :]
+    head_out[...] = error * pooled
+    pred_out[...] = jnp.sum(jnp.where(eye(4), predicted, 0.0), axis=0, keepdims=True)
 
     arrive(6, h_2, group)
-    high_out[...] = add_up(h_2, group)
+    h_tall[...] = jnp.transpose(add_up(h_2, group))
+    for t in range(27):
+        high_out[t] = h_tall[4 * t:4 * t + 4, :]
+    high_bias[...] = h_tall[108:109, :]
     c_bg.wait_recv()
     for copy in copies:
         copy.wait_send()
@@ -483,49 +553,56 @@
         pltpu.make_async_copy(ref, ref, ss.at[stage]).wait()
 
 
+def finish(*refs):
+    sources, results, sem = refs[:7], refs[7:14], refs[14]
+    moves = [pltpu.make_async_copy(a, b, sem.at[n]) for n, (a, b) in enumerate(zip(sources, results))]
+    for move in moves:
+        move.start()
+    for move in moves:
+        move.wait()
+
+
 def shards(nx, ny, volume, weight_high, bias_high, weight_low, bias_low, head_weight, head_bias, targets):
     cells = 2 * nx * 16 * ny * 64
-    wh = jnp.transpose(weight_high, (0, 2, 3, 4, 1))
-    wh = jnp.pad(wh, ((0, 0), (0, 0), (0, 0), (0, 1), (0, 0))).reshape(16, 3, 3, 16)
-    w1 = jnp.concatenate(
-        [
-            jnp.pad(wh, ((0, 0), (0, 0), (0, 2), (0, 0))).reshape(16, 240),
-            jnp.pad(wh, ((0, 0), (0, 0), (2, 0), (0, 0))).reshape(16, 240),
-        ],
-        axis=0,
+    small = (
+        jnp.transpose(weight_high, (2, 3, 4, 1, 0)).reshape(27, 4, 16),
+        jnp.transpose(weight_low, (2, 3, 4, 1, 0)).reshape(432, 32),
+        bias_high[None],
+        bias_low[None],
+        head_weight.T,
+        head_bias[None],
+        targets[None],
     )
-    wl = jnp.transpose(weight_low, (0, 2, 3, 4, 1)).reshape(32, 432)
-    wt = jnp.transpose(weight_low, (1, 2, 3, 4, 0))
-    wt = jnp.pad(wt, ((0, 0), (0, 1), (0, 1), (0, 0), (0, 0)))
-    tap = ((1, 3), (2, 0))
-    wb = jnp.stack(
-        [
-            jnp.stack([wt[:, tap[sx][dx], tap[sy][dy]] for dx in range(2) for dy in range(2)], axis=1)
-            for sx in range(2)
-            for sy in range(2)
-        ],
-        axis=0,
-    ).reshape(64, 384)
-    b1 = jnp.concatenate([bias_high, bias_high])[:, None]
-    makers = (depth_taps, rows_to_channels, depth_taps_low, depth_spread, channels_to_rows, low_order, high_order)
-    tables = [jnp.asarray(t().astype(np.float32), BF) for t in makers]
+    tables = [jnp.asarray(t(), BF) for t in (early_tables, late_tables)]
     vm = pl.BlockSpec(memory_space=pltpu.VMEM)
+    hbm = pl.BlockSpec(memory_space=pltpu.HBM)
     dma = pltpu.SemaphoreType.DMA
     per = 16 // nx
     group = 2 * ny
-    bg, pred, head, low, low_bias, high = pl.pallas_call(
+    results = (
+        jax.ShapeDtypeStruct((16, 4, 32, 128), BF),
+        jax.ShapeDtypeStruct((1, 4), F32),
+        jax.ShapeDtypeStruct((4, 32), F32),
+        jax.ShapeDtypeStruct((432, 32), F32),
+        jax.ShapeDtypeStruct((1, 32), F32),
+        jax.ShapeDtypeStruct((27, 4, 16), F32),
+        jax.ShapeDtypeStruct((1, 16), F32),
+    )
+    outs = pl.pallas_call(
         functools.partial(kernel, nx, ny, cells),
-        out_shape=(
-            jax.ShapeDtypeStruct((16, 4, 32, 128), BF),
-            jax.ShapeDtypeStruct((1, 4), F32),
-            jax.ShapeDtypeStruct((32, 4), F32),
-            jax.ShapeDtypeStruct((32, 432), F32),
-            jax.ShapeDtypeStruct((32, 1), F32),
-            jax.ShapeDtypeStruct((16, 128), F32),
-        ),
-        in_specs=[vm] * 16,
-        out_specs=(vm,) * 6,
+        out_shape=results,
+        in_specs=[hbm] * 10,
+        out_specs=(vm,) * 7,
         scratch_shapes=[
+            pltpu.VMEM((4, 4, 64, 256), BF),
+            pltpu.VMEM((256, 896), BF),
+            pltpu.VMEM((256, 1024), BF),
+            *(pltpu.VMEM(a.shape, a.dtype) for a in small),
+            pltpu.VMEM((128, 16), F32),
+            pltpu.VMEM((32, 432), BF),
+            pltpu.VMEM((64, 384), BF),
+            pltpu.VMEM((128, 16), F32),
+            dma((10,)),
             pltpu.VMEM((4, 64, 256), BF),
             pltpu.VMEM((5, 1040, 128), BF),
             pltpu.VMEM((2, 512, 128), F32),
@@ -552,17 +629,23 @@
             collective_id=0, has_side_effects=True, vmem_limit_bytes=48 << 20
         ),
         name="fused",
-    )(
-        volume, w1, b1, wl, bias_low[:, None], head_weight, head_bias[None], targets[None], wb, *tables
-    )
+    )(volume, *tables, *small)
+    bg, pred, head, low, low_bias, high, high_bias = pl.pallas_call(
+        finish,
+        out_shape=results,
+        in_specs=[vm] * 7,
+        out_specs=(hbm,) * 7,
+        scratch_shapes=[dma((7,))],
+        name="finish",
+    )(*outs)
     return (
         pred[0],
         bg,
-        high[:, :108].reshape(16, 4, 3, 3, 3),
-        high[:, 108],
-        low.reshape(32, 16, 3, 3, 3),
-        low_bias[:, 0],
-        head,
+        jnp.transpose(high.reshape(3, 3, 3, 4, 16), (4, 3, 0, 1, 2)),
+        high_bias[0],
+        jnp.transpose(low.reshape(3, 3, 3, 16, 32), (4, 3, 0, 1, 2)),
+        low_bias[0],
+        head.T,
     )
 
 

time: 56.3 us -> 55.1 us (0.979)
  Pallas kernels: 45.3 us -> 44 us
  local copies, waits for them, and re-layouts: 9.1 us -> 9.99 us
  other arithmetic: 0.81 us -> 0 us
    unnamed x32 -> x34, local copies, waits for them, and re-layouts: 4.56 us -> 9.99 us
    reshape x7 -> x0, local copies, waits for them, and re-layouts: 1.61 us -> none  [the longest x1 0.97 us: shards(): wl = jnp.transpose(weight_low, (0, 2, 3, 4, 1)).reshape(32, 432)]
    pallas_call x1 -> x2, Pallas kernels: 45.3 us -> 44 us  [the longest x1 41.9 us: shards(): pl.pallas_call(functools.partial(kernel, nx, ny, cells), out_shape=result...]
    another operation x3 -> x0, local copies, waits for them, and re-layouts: 0.96 us -> none  [the longest x2 0.86 us: shards(): jnp.stack([wt[:, tap[sx][dx], tap[sy][dy]] for dx in range(2) for dy in r...]
    pad x2 -> x0, local copies, waits for them, and re-layouts: 0.87 us -> none  [the longest x1 0.8 us: shards(): jnp.pad(wh, ((0, 0), (0, 0), (0, 0), (0, 1), (0, 0))).reshape(16, 3, 3, 16)]
    slice x2 -> x0, local copies, waits for them, and re-layouts: 0.8 us -> none  [the longest x1 0.69 us: shards(): high[:, 108]]
    pallas_call x1 -> x0, other arithmetic: 0.63 us -> none  [shards(): pl.pallas_call(functools.partial(kernel, nx, ny, cells), out_shape=(jax.S...]
where the time goes in v3:
time: 55.1 us; the launch traced here: 54.7 us
  Pallas kernels  44 us (80%)
  local copies, waits for them, and re-layouts  9.99 us (18%)
  between operations  0.71 us (1%)
    pallas_call x1, Pallas kernels, shards(): pl.pallas_call(functools.partial(kernel, nx, ny, cells), out_shape=result...  41.9 us
    unnamed x34, local copies, waits for them, and re-layouts  9.99 us
    pallas_call x1, Pallas kernels, shards(): pl.pallas_call(finish, out_shape=results, in_specs=[vm] * 7, out_specs=(h...  2.14 us

profile of v3, /device:TPU:1, one launch (start us, length us, event | category | flops | bytes accessed | tf_op | source)
XLA Modules:
  0.0 54.7 jit_solution(453085129819462803)
XLA Ops:
  0.6 0.0 copy-start.13
  0.6 0.0 copy-start.8
  0.7 0.0 copy-start.10
  0.7 0.0 copy-start.11
  0.7 0.0 copy-start.12
  0.7 0.6 %copy-done.13 = f32[4]{0:T(128)S(1)} copy-done((f32[4]{0:T(128)S(1)}, f32[4]{0:T(128)}, u32[]{:S(2)}) %copy-start.13) | copy-done | bytes 40
  1.3 0.0 copy-done.8
  1.3 0.0 copy-done.10
  1.3 0.0 copy-done.11
  1.3 0.0 copy-done.12
  1.4 0.0 copy-start
  1.4 1.2 %copy-done = bf16[4,8,64,256]{3,2,1,0:T(8,128)(2,1)S(1)} copy-done((bf16[4,8,64,256]{3,2,1,0:T(8,128)(2,1)S(1)}, bf16[4,8,64,256]{3,2,1,0:T(8,128)(2,1)}, u32[]{:S(2)}) %copy-start) | copy-done | bytes 1048600
  2.6 0.0 copy-start.1
  2.6 1.0 %copy-done.1 = bf16[256,1024]{1,0:T(8,128)(2,1)S(1)} copy-done((bf16[256,1024]{1,0:T(8,128)(2,1)S(1)}, bf16[256,1024]{1,0:T(8,128)(2,1)}, u32[]{:S(2)}) %copy-start.1) | copy-done | bytes 524312
  3.6 0.0 copy-start.3
  3.6 1.0 %copy-done.3 = bf16[256,896]{1,0:T(8,128)(2,1)S(1)} copy-done((bf16[256,896]{1,0:T(8,128)(2,1)S(1)}, bf16[256,896]{1,0:T(8,128)(2,1)}, u32[]{:S(2)}) %copy-start.3) | copy-done | bytes 458776
  4.6 0.0 copy-start.5
  4.6 0.9 %copy-done.5 = bf16[32,16,3,3,3]{0,1,4,3,2:T(8,128)(2,1)S(1)} copy-done((bf16[32,16,3,3,3]{0,1,4,3,2:T(8,128)(2,1)S(1)}, bf16[32,16,3,3,3]{0,1,4,3,2:T(8,128)(2,1)}, u32[]{:S(2)}) %copy-start.5) | copy-done | bytes 27672
  5.5 0.0 copy-start.7
  5.5 0.7 %copy-done.7 = bf16[16,4,3,3,3]{0,1,4,3,2:T(4,128)(2,1)S(1)} copy-done((bf16[16,4,3,3,3]{0,1,4,3,2:T(4,128)(2,1)S(1)}, bf16[16,4,3,3,3]{0,1,4,3,2:T(4,128)(2,1)}, u32[]{:S(2)}) %copy-start.7) | copy-done | bytes 3480
  6.3 41.9 %fused.1 = (bf16[16,4,32,128]{3,2,1,0:T(8,128)(2,1)S(1)}, f32[1,4]{1,0:T(1,128)S(1)}, f32[4,32]{1,0:T(4,128)S(1)}, f32[432,32]{1,0:T(8,128)S(1)}, f32[1,32]{1,0:...) custom-call(bf16[4,8,64,256]{3,2,1,0:T(8,128)(2,1)S(1)} %copy-done, bf16[256,896]{1,0:T(8,128)(2,1)S(1)} %copy-done.3, ...), custom_call_target="tpu_custom_call" | custom-call | tf_op jit(solution)/shard_map/fused/pallas_call | solution.py:591
  48.2 0.0 copy-start.2
  48.2 0.8 %copy-done.2 = bf16[16,4,32,128]{3,2,1,0:T(8,128)(2,1)} copy-done((bf16[16,4,32,128]{3,2,1,0:T(8,128)(2,1)}, bf16[16,4,32,128]{3,2,1,0:T(8,128)(2,1)S(1)}, u32[]{:S(2)}) %copy-start.2) | copy-done | bytes 524312
  49.0 0.0 copy-start.4
  49.0 0.7 %copy-done.4 = f32[432,32]{1,0:T(8,128)} copy-done((f32[432,32]{1,0:T(8,128)}, f32[432,32]{1,0:T(8,128)S(1)}, u32[]{:S(2)}) %copy-start.4) | copy-done | bytes 55320
  49.7 0.0 copy-start.6
  49.7 0.6 %copy-done.6 = f32[27,4,16]{2,1,0:T(4,128)} copy-done((f32[27,4,16]{2,1,0:T(4,128)}, f32[27,4,16]{2,1,0:T(4,128)S(1)}, u32[]{:S(2)}) %copy-start.6) | copy-done | bytes 6936
  50.3 0.0 copy-start.14
  50.3 0.6 %copy-done.14 = f32[1,4]{1,0:T(1,128)} copy-done((f32[1,4]{1,0:T(1,128)}, f32[1,4]{1,0:T(1,128)S(1)}, u32[]{:S(2)}) %copy-start.14) | copy-done | bytes 40
  50.9 0.0 copy-start.15
  50.9 0.5 copy-done.15
  51.4 0.0 copy-start.16
  51.4 0.6 %copy-done.16 = f32[1,16]{1,0:T(1,128)} copy-done((f32[1,16]{1,0:T(1,128)}, f32[1,16]{1,0:T(1,128)S(1)}, u32[]{:S(2)}) %copy-start.16) | copy-done | bytes 88
  52.0 0.0 copy-start.9
  52.0 0.6 %copy-done.9 = f32[4,32]{1,0:T(4,128)} copy-done((f32[4,32]{1,0:T(4,128)}, f32[4,32]{1,0:T(4,128)S(1)}, u32[]{:S(2)}) %copy-start.9) | copy-done | bytes 536
  52.6 2.1 %finish.1 = (bf16[16,4,32,128]{3,2,1,0:T(8,128)(2,1)}, f32[1,4]{1,0:T(1,128)}, f32[4,32]{1,0:T(4,128)}, f32[432,32]{1,0:T(8,128)}, f32[1,32]{1,0:T(1,128)}, /*index=5*/f32[27,4,16]{2,1,0:T(4,128)}, f32[1,16]{1,0:T(1,128)}) custom-call(bf16[16,4,32,128]{3,2,1,0:T(8,128)(2,1)} %copy-done.2, f32[1,4]{1,0:T(1,128)} %copy-done.14, f32[4,32]{1,0:T(4,128)} %copy-done.9, ...), custom_call_target="tpu_custom_call" | custom-call | tf_op jit(solution)/shard_map/finish/pallas_call | solution.py:633
Async XLA Ops:
  0.6 0.7 %copy-start.13 = (f32[4]{0:T(128)S(1)}, f32[4]{0:T(128)}, u32[]{:S(2)}) copy-start(f32[4]{0:T(128)} %param.17) | copy-start | bytes 52
  0.6 0.7 %copy-start.8 = (f32[32,4]{0,1:T(4,128)S(1)}, f32[32,4]{0,1:T(4,128)}, u32[]{:S(2)}) copy-start(f32[32,4]{0,1:T(4,128)} %param.15) | copy-start | bytes 1540
  0.7 0.7 %copy-start.10 = (f32[16]{0:T(128)S(1)}, f32[16]{0:T(128)}, u32[]{:S(2)}) copy-start(f32[16]{0:T(128)} %param.12) | copy-start | bytes 196
  0.7 0.7 %copy-start.11 = (f32[32]{0:T(128)S(1)}, f32[32]{0:T(128)}, u32[]{:S(2)}) copy-start(f32[32]{0:T(128)} %param.14) | copy-start | bytes 388
  0.7 0.7 %copy-start.12 = (f32[4]{0:T(128)S(1)}, f32[4]{0:T(128)}, u32[]{:S(2)}) copy-start(f32[4]{0:T(128)} %param.16) | copy-start | bytes 52
  1.4 1.2 %copy-start = (bf16[4,8,64,256]{3,2,1,0:T(8,128)(2,1)S(1)}, bf16[4,8,64,256]{3,2,1,0:T(8,128)(2,1)}, u32[]{:S(2)}) copy-start(bf16[4,8,64,256]{3,2,1,0:T(8,128)(2,1)} %v_hbm.1) | copy-start | bytes 3145732
  2.6 1.0 %copy-start.1 = (bf16[256,1024]{1,0:T(8,128)(2,1)S(1)}, bf16[256,1024]{1,0:T(8,128)(2,1)}, u32[]{:S(2)}) copy-start(bf16[256,1024]{1,0:T(8,128)(2,1)} %constant.5.clone.tb_hbm) | copy-start | bytes 1572868
  3.6 1.0 %copy-start.3 = (bf16[256,896]{1,0:T(8,128)(2,1)S(1)}, bf16[256,896]{1,0:T(8,128)(2,1)}, u32[]{:S(2)}) copy-start(bf16[256,896]{1,0:T(8,128)(2,1)} %constant.4.clone.ta_hbm) | copy-start | bytes 1376260
  4.6 0.9 %copy-start.5 = (bf16[32,16,3,3,3]{0,1,4,3,2:T(8,128)(2,1)S(1)}, bf16[32,16,3,3,3]{0,1,4,3,2:T(8,128)(2,1)}, u32[]{:S(2)}) copy-start(bf16[32,16,3,3,3]{0,1,4,3,2:T(8,128)(2,1)} %param.13) | copy-start | bytes 82948
  5.5 0.7 %copy-start.7 = (bf16[16,4,3,3,3]{0,1,4,3,2:T(4,128)(2,1)S(1)}, bf16[16,4,3,3,3]{0,1,4,3,2:T(4,128)(2,1)}, u32[]{:S(2)}) copy-start(bf16[16,4,3,3,3]{0,1,4,3,2:T(4,128)(2,1)} %param.11) | copy-start | bytes 10372
  48.2 0.8 %copy-start.2 = (bf16[16,4,32,128]{3,2,1,0:T(8,128)(2,1)}, bf16[16,4,32,128]{3,2,1,0:T(8,128)(2,1)S(1)}, u32[]{:S(2)}) copy-start(bf16[16,4,32,128]{3,2,1,0:T(8,128)(2,1)S(1)} %get-tuple-element.21.refs_0_) | copy-start | bytes 1572868
  49.0 0.7 %copy-start.4 = (f32[432,32]{1,0:T(8,128)}, f32[432,32]{1,0:T(8,128)S(1)}, u32[]{:S(2)}) copy-start(f32[432,32]{1,0:T(8,128)S(1)} %get-tuple-element.24.refs_3_) | copy-start | bytes 165892
  49.7 0.6 %copy-start.6 = (f32[27,4,16]{2,1,0:T(4,128)}, f32[27,4,16]{2,1,0:T(4,128)S(1)}, u32[]{:S(2)}) copy-start(f32[27,4,16]{2,1,0:T(4,128)S(1)} %get-tuple-element.26.refs_5_) | copy-start | bytes 20740
  50.3 0.6 %copy-start.14 = (f32[1,4]{1,0:T(1,128)}, f32[1,4]{1,0:T(1,128)S(1)}, u32[]{:S(2)}) copy-start(f32[1,4]{1,0:T(1,128)S(1)} %get-tuple-element.22.refs_1_) | copy-start | bytes 52
  50.9 0.5 copy-start.15
  51.4 0.6 %copy-start.16 = (f32[1,16]{1,0:T(1,128)}, f32[1,16]{1,0:T(1,128)S(1)}, u32[]{:S(2)}) copy-start(f32[1,16]{1,0:T(1,128)S(1)} %get-tuple-element.27.refs_6_) | copy-start | bytes 196
  52.0 0.6 %copy-start.9 = (f32[4,32]{1,0:T(4,128)}, f32[4,32]{1,0:T(4,128)S(1)}, u32[]{:S(2)}) copy-start(f32[4,32]{1,0:T(4,128)S(1)} %get-tuple-element.23.refs_2_) | copy-start | bytes 1540

commit v4 on v3

--- a/solution.py
+++ b/solution.py
@@ -116,11 +116,11 @@
     nx, ny, cells,
     v_hbm, ta_hbm, tb_hbm, *rest,
 ):
-    small_hbm, rest = rest[:7], rest[7:]
+    small_hbm, results, rest = rest[:7], rest[7:14], rest[14:]
     (
         bg_out, pred_out, head_out, low_out, low_bias, high_out, high_bias,
         v, ta, tb, wh, wlt, bh_row, bl_row, hw, hb_row, tg_row,
-        w_tall, wl, wb, h_tall, ls,
+        w_tall, wl, wb, h_tall, ls, os,
         halo, a1, pre, act, taps, slope, slope_y, up, grad_b,
         pool_s, pool_1, pool_2, gsend, g_1, g_2s, g_2, g_3, h_s, h_1, h_2,
         hs, hr, ss, rs,
@@ -170,6 +170,11 @@
     for peer in partners:
         pl.semaphore_signal(barrier, inc=1, device_id=peer, device_id_type=MESH)
 
+    def deliver(n, ref):
+        move = pltpu.make_async_copy(ref, results[n], os.at[n])
+        move.start()
+        return move
+
     copies = []
 
     def send(n, src, dst, peer):
@@ -473,6 +478,8 @@
     predicted = jnp.sum(weight * pooled, axis=1, keepdims=True) + to_column(hb_row[...])
     error = predicted - to_column(tg_row[...])
     signal = jnp.sum(weight * error, axis=0, keepdims=True)
+    head_out[...] = error * pooled
+    pred_out[...] = jnp.sum(jnp.where(eye(4), predicted, 0.0), axis=0, keepdims=True)
     weights = (wb[...].astype(F32) * jnp.concatenate([signal] * 12, axis=1)).astype(BF)
 
     def high_back(t, carry):
@@ -537,25 +544,30 @@
     g_all = jnp.transpose(jnp.concatenate(bands, axis=0)) * (signal * scale)
     low_out[...] = g_all[0:432, :]
     low_bias[...] = g_all[432:433, :]
-    head_out[...] = error * pooled
-    pred_out[...] = jnp.sum(jnp.where(eye(4), predicted, 0.0), axis=0, keepdims=True)
+    moves = [deliver(n, ref) for n, ref in ((3, low_out), (4, low_bias), (2, head_out), (1, pred_out))]
+    c_bg.wait_recv()
+    moves.append(deliver(0, bg_out))
 
     arrive(6, h_2, group)
     h_tall[...] = jnp.transpose(add_up(h_2, group))
     for t in range(27):
         high_out[t] = h_tall[4 * t:4 * t + 4, :]
     high_bias[...] = h_tall[108:109, :]
-    c_bg.wait_recv()
+    moves += [deliver(5, high_out), deliver(6, high_bias)]
     for copy in copies:
         copy.wait_send()
     for stage, buffer, n in stages:
         ref = buffer.at[pl.ds(0, n - 1)]
         pltpu.make_async_copy(ref, ref, ss.at[stage]).wait()
+    for move in moves:
+        move.wait()
 
 
 def finish(*refs):
     sources, results, sem = refs[:7], refs[7:14], refs[14]
-    moves = [pltpu.make_async_copy(a, b, sem.at[n]) for n, (a, b) in enumerate(zip(sources, results))]
+    pairs = [(sources[0].at[pl.ds(4 * n, 4)], results[0].at[pl.ds(4 * n, 4)]) for n in range(4)]
+    pairs += list(zip(sources[1:], results[1:]))
+    moves = [pltpu.make_async_copy(a, b, sem.at[n]) for n, (a, b) in enumerate(pairs)]
     for move in moves:
         move.start()
     for move in moves:
@@ -592,8 +604,9 @@
         functools.partial(kernel, nx, ny, cells),
         out_shape=results,
         in_specs=[hbm] * 10,
-        out_specs=(vm,) * 7,
+        out_specs=(hbm,) * 7,
         scratch_shapes=[
+            *(pltpu.VMEM(a.shape, a.dtype) for a in results),
             pltpu.VMEM((4, 4, 64, 256), BF),
             pltpu.VMEM((256, 896), BF),
             pltpu.VMEM((256, 1024), BF),
@@ -603,6 +616,7 @@
             pltpu.VMEM((64, 384), BF),
             pltpu.VMEM((128, 16), F32),
             dma((10,)),
+            dma((7,)),
             pltpu.VMEM((4, 64, 256), BF),
             pltpu.VMEM((5, 1040, 128), BF),
             pltpu.VMEM((2, 512, 128), F32),
@@ -626,7 +640,7 @@
             dma((10,)), dma((10,)), dma((7,)), dma((7,)),
         ],
         compiler_params=pltpu.CompilerParams(
-            collective_id=0, has_side_effects=True, vmem_limit_bytes=48 << 20
+            collective_id=0, has_side_effects=True, vmem_limit_bytes=64 << 20
         ),
         name="fused",
     )(volume, *tables, *small)
@@ -635,7 +649,8 @@
         out_shape=results,
         in_specs=[vm] * 7,
         out_specs=(hbm,) * 7,
-        scratch_shapes=[dma((7,))],
+        scratch_shapes=[dma((10,))],
+        compiler_params=pltpu.CompilerParams(vmem_limit_bytes=64 << 20),
         name="finish",
     )(*outs)
     return (

time: 55.1 us -> 45.7 us (0.83)
  local copies, waits for them, and re-layouts: 9.99 us -> 0 us
  Pallas kernels: 44 us -> 45 us
    unnamed x34 -> x0, local copies, waits for them, and re-layouts: 9.99 us -> none
    pallas_call x1, Pallas kernels: 41.9 us -> 42.8 us  [shards(): pl.pallas_call(functools.partial(kernel, nx, ny, cells), out_shape=result...]
where the time goes in v4:
time: 45.7 us; the launch traced here: 45.6 us
  Pallas kernels  45 us (98%)
  between operations  0.64 us (1%)
    pallas_call x1, Pallas kernels, shards(): pl.pallas_call(functools.partial(kernel, nx, ny, cells), out_shape=result...  42.8 us
    pallas_call x1, Pallas kernels, shards(): pl.pallas_call(finish, out_shape=results, in_specs=[vm] * 7, out_specs=(h...  2.17 us

profile of v4, /device:TPU:1, one launch (start us, length us, event | category | flops | bytes accessed | tf_op | source)
XLA Modules:
  0.0 45.6 jit_solution(4272130604677203342)
XLA Ops:
  0.6 42.8 %fused.1 = (bf16[16,4,32,128]{3,2,1,0:T(8,128)(2,1)}, f32[1,4]{1,0:T(1,128)}, f32[4,32]{1,0:T(4,128)}, f32[432,32]{1,0:T(8,128)}, f32[1,32]{1,0:T(1,128)}, /*index=5*/f32[27,4,16]{2,1,0:T(4,128)}, f32[1,16]{1,0:T(1,128)}) custom-call(bf16[4,8,64,256]{3,2,1,0:T(8,128)(2,1)} %v_hbm.1, bf16[256,896]{1,0:T(8,128)(2,1)} %constant.4.clone.ta_hbm, ...), custom_call_target="tpu_custom_call" | custom-call | tf_op jit(solution)/shard_map/fused/pallas_call | solution.py:603
  43.4 2.2 %finish.1 = (bf16[16,4,32,128]{3,2,1,0:T(8,128)(2,1)}, f32[1,4]{1,0:T(1,128)}, f32[4,32]{1,0:T(4,128)}, f32[432,32]{1,0:T(8,128)}, f32[1,32]{1,0:T(1,128)}, /*index=5*/f32[27,4,16]{2,1,0:T(4,128)}, f32[1,16]{1,0:T(1,128)}) custom-call(bf16[16,4,32,128]{3,2,1,0:T(8,128)(2,1)} %get-tuple-element.21.refs_0_, f32[1,4]{1,0:T(1,128)} %get-tuple-element.22.refs_1_, ...), custom_call_target="tpu_custom_call" | custom-call | tf_op jit(solution)/shard_map/finish/pallas_call | solution.py:647

commit v5 on v4

--- a/solution.py
+++ b/solution.py
@@ -11,7 +11,7 @@
 MESH = pl.DeviceIdType.MESH
 BF = jnp.bfloat16
 F32 = jnp.float32
-UNROLL = (8, 4, 2, 4, 4, 4, 4, 4, 8, 4)
+UNROLL = (8, 4, 1, 4, 4, 4, 4, 4, 8, 4)
 
 
 def depth_taps():
@@ -215,7 +215,7 @@
             parts.append(jnp.concatenate([d[:, 0:128], d[:, 128:256], d[:, 256:384]], axis=0))
         out = mm(ta[:, 384:576], jnp.concatenate(parts, axis=1)).astype(BF)
         for h in range(2):
-            start = pl.multiple_of(16 + (yb * 2 + h) * 256, 16)
+            start = pl.multiple_of(48 + (yb * 2 + h) * 256, 16)
             a1[xs, pl.ds(start, 256), :] = out[:, h * 128:(h + 1) * 128]
 
     def own_plane(t, carry):
@@ -256,14 +256,16 @@
 
     pl.semaphore_wait(barrier, len(partners))
 
-    c_raw = send(0, v.at[:, 3], halo, xu)
-    c_a1y = send(1, a1.at[pl.ds(1, 4), pl.ds(1024, 16)], a1.at[pl.ds(1, 4), pl.ds(0, 16)], {"gy": yu})
-    c_a1c = send(2, a1.at[4, pl.ds(1024, 16)], a1.at[0, pl.ds(0, 16)], {**xu, "gy": yu})
+    c_raw = [
+        send(5 * n, v.at[:, 3, pl.ds(32 * n, 32)], halo.at[:, pl.ds(32 * n, 32)], xu) for n in range(2)
+    ]
+    c_a1y = send(1, a1.at[pl.ds(1, 4), pl.ds(1024, 48)], a1.at[pl.ds(1, 4), pl.ds(0, 48)], {"gy": yu})
+    c_a1c = send(2, a1.at[4, pl.ds(1024, 48)], a1.at[0, pl.ds(0, 48)], {**xu, "gy": yu})
 
     def conv_high(px, t):
         cols = []
         for h in range(2):
-            start = pl.multiple_of(t * 128 + h * 64, 16)
+            start = pl.multiple_of(32 + t * 128 + h * 64, 16)
             cols.append(jnp.concatenate([a1[2 * px + k, pl.ds(start, 80), :] for k in range(3)], axis=0))
         out = mm(w1, jnp.concatenate(cols, axis=1)) + b1
         acts = (out * sigmoid(out)).astype(BF)
@@ -272,6 +274,12 @@
             start = pl.multiple_of(16 + t * 64 + h * 32, 16)
             act[px + 1, pl.ds(start, 32), :] = acts[:, h * 128:(h + 1) * 128]
 
+    def conv_edge(px):
+        cols = jnp.concatenate([a1[2 * px + k, 0:80, :] for k in range(3)], axis=0)
+        out = (mm(w1, cols) + b1)[0:16]
+        acts = (out * sigmoid(out)).astype(BF)
+        act[px + 1, 0:16, :] = jnp.where(my == 0, jnp.zeros_like(acts), acts)
+
     def conv_high_1(t, carry):
         conv_high(1, t)
         return carry
@@ -279,40 +287,6 @@
     def conv_high_0(t, carry):
         conv_high(0, t)
         return carry
-
-    lax.fori_loop(1, 8, conv_high_1, 0, unroll=UNROLL[1])
-    c_a1y.wait_recv()
-
-    @pl.when(my == 0)
-    def _():
-        a1[1:5, 0:16, :] = jnp.zeros((4, 16, 128), BF)
-
-    conv_high(1, 0)
-    c_ax = send(3, act.at[2, pl.ds(16, 512)], act.at[0, pl.ds(16, 512)], xu)
-    c_ac = send(4, act.at[2, pl.ds(512, 16)], act.at[0, pl.ds(0, 16)], {**xu, "gy": yu})
-    c_raw.wait_recv()
-
-    @pl.when(first_x)
-    def _():
-        halo[...] = jnp.zeros_like(halo)
-
-    def halo_plane(yb, carry):
-        def load(b):
-            return halo[:, pl.ds(pl.multiple_of(b * 16, 16), 16), :]
-
-        to_channels(load, 0, yb)
-        return carry
-
-    lax.fori_loop(0, 2, halo_plane, 0, unroll=UNROLL[2])
-    c_a1c.wait_recv()
-
-    @pl.when(jnp.logical_or(first_x, my == 0))
-    def _():
-        a1[0, 0:16, :] = jnp.zeros((16, 128), BF)
-
-    conv_high(0, 7)
-    c_ay = send(5, act.at[pl.ds(1, 2), pl.ds(512, 16)], act.at[pl.ds(1, 2), pl.ds(0, 16)], {"gy": yu})
-    lax.fori_loop(0, 7, conv_high_0, 0, unroll=UNROLL[1])
 
     def to_taps(xs, first, count):
         low = act[xs, pl.ds(pl.multiple_of(16 * first, 16), 16 * count), :]
@@ -323,32 +297,54 @@
                 row = pl.multiple_of(((first + t) * 3 + k) * 16, 16)
                 taps[xs, pl.ds(row, 16), :] = d[16 * t:16 * (t + 1), 128 * k:128 * (k + 1)]
 
-    def taps_own(t, carry):
-        to_taps(1 + t // 4, 1 + 4 * lax.rem(t, 4), 4)
-        return carry
-
-    def taps_halo(t, carry):
-        to_taps(0, 1 + 4 * t, 4)
-        return carry
-
-    lax.fori_loop(0, 8, taps_own, 0, unroll=UNROLL[3])
-    c_ay.wait_recv()
-    c_ac.wait_recv()
+    def all_taps(xs):
+        def body(t, carry):
+            to_taps(xs, 1 + 4 * t, 4)
+            return carry
+
+        lax.fori_loop(0, 4, body, 0, unroll=UNROLL[3])
+        to_taps(xs, 0, 1)
+
+    lax.fori_loop(1, 8, conv_high_1, 0, unroll=UNROLL[1])
+    c_ax = [send(3, act.at[2, pl.ds(80, 448)], act.at[0, pl.ds(80, 448)], xu)]
+    c_a1y.wait_recv()
 
     @pl.when(my == 0)
     def _():
-        act[:, 0:16, :] = jnp.zeros((3, 16, 128), BF)
-
-    to_taps(1, 0, 1)
-    to_taps(2, 0, 1)
-    c_ax.wait_recv()
+        a1[1:5, 0:48, :] = jnp.zeros((4, 48, 128), BF)
+
+    conv_high(1, 0)
+    conv_edge(1)
+    c_ax.append(send(4, act.at[2, pl.ds(0, 80)], act.at[0, pl.ds(0, 80)], xu))
+    all_taps(2)
+    c_a1c.wait_recv()
+
+    @pl.when(jnp.logical_or(first_x, my == 0))
+    def _():
+        a1[0, 0:48, :] = jnp.zeros((48, 128), BF)
+
+    for n in range(2):
+        c_raw[n].wait_recv()
+
+        @pl.when(first_x)
+        def _():
+            halo[:, 32 * n:32 * n + 32, :] = jnp.zeros((4, 32, 256), BF)
+
+        def load(b):
+            return halo[:, 16 * b:16 * b + 16, :]
+
+        to_channels(load, 0, n)
+        lax.fori_loop(4 * n, 4 * n + 4, conv_high_0, 0, unroll=UNROLL[1])
+    conv_edge(0)
+    all_taps(1)
+    for copy in c_ax:
+        copy.wait_recv()
 
     @pl.when(first_x)
     def _():
         act[0] = jnp.zeros((528, 128), BF)
 
-    to_taps(0, 0, 1)
-    lax.fori_loop(0, 4, taps_halo, 0, unroll=UNROLL[3])
+    all_taps(0)
 
     def window(j):
         start = pl.multiple_of(j * 96, 16)
@@ -492,7 +488,7 @@
         ws, ups = [], []
         for h in range(2):
             at = pl.ds(pl.multiple_of(t * 64 + h * 32, 32), 32)
-            begin = pl.multiple_of(t * 128 + h * 64, 16)
+            begin = pl.multiple_of(32 + t * 128 + h * 64, 16)
             for qx in range(2):
                 tile = out[32 * qx:32 * (qx + 1), h * 128:(h + 1) * 128]
                 grad_b[qx, at, :] = tile
@@ -618,7 +614,7 @@
             dma((10,)),
             dma((7,)),
             pltpu.VMEM((4, 64, 256), BF),
-            pltpu.VMEM((5, 1040, 128), BF),
+            pltpu.VMEM((5, 1072, 128), BF),
             pltpu.VMEM((2, 512, 128), F32),
             pltpu.VMEM((3, 528, 128), BF),
             pltpu.VMEM((3, 816, 128), BF),

time: 45.7 us -> 43.6 us (0.954)
  Pallas kernels: 45 us -> 42.9 us
    pallas_call x1, Pallas kernels: 42.8 us -> 40.7 us  [shards(): pl.pallas_call(functools.partial(kernel, nx, ny, cells), out_shape=result...]
where the time goes in v5:
time: 43.6 us; the launch traced here: 43.5 us
  Pallas kernels  42.9 us (98%)
  between operations  0.64 us (1%)
    pallas_call x1, Pallas kernels, shards(): pl.pallas_call(functools.partial(kernel, nx, ny, cells), out_shape=result...  40.7 us
    pallas_call x1, Pallas kernels, shards(): pl.pallas_call(finish, out_shape=results, in_specs=[vm] * 7, out_specs=(h...  2.17 us

profile of v5, /device:TPU:1, one launch (start us, length us, event | category | flops | bytes accessed | tf_op | source)
XLA Modules:
  0.0 43.5 jit_solution(8581552564154389453)
XLA Ops:
  0.6 40.7 %fused.1 = (bf16[16,4,32,128]{3,2,1,0:T(8,128)(2,1)}, f32[1,4]{1,0:T(1,128)}, f32[4,32]{1,0:T(4,128)}, f32[432,32]{1,0:T(8,128)}, f32[1,32]{1,0:T(1,128)}, /*index=5*/f32[27,4,16]{2,1,0:T(4,128)}, f32[1,16]{1,0:T(1,128)}) custom-call(bf16[4,8,64,256]{3,2,1,0:T(8,128)(2,1)} %v_hbm.1, bf16[256,896]{1,0:T(8,128)(2,1)} %constant.4.clone.ta_hbm, ...), custom_call_target="tpu_custom_call" | custom-call | tf_op jit(solution)/shard_map/fused/pallas_call | solution.py:599
  41.3 2.2 %finish.1 = (bf16[16,4,32,128]{3,2,1,0:T(8,128)(2,1)}, f32[1,4]{1,0:T(1,128)}, f32[4,32]{1,0:T(4,128)}, f32[432,32]{1,0:T(8,128)}, f32[1,32]{1,0:T(1,128)}, /*index=5*/f32[27,4,16]{2,1,0:T(4,128)}, f32[1,16]{1,0:T(1,128)}) custom-call(bf16[16,4,32,128]{3,2,1,0:T(8,128)(2,1)} %get-tuple-element.21.refs_0_, f32[1,4]{1,0:T(1,128)} %get-tuple-element.22.refs_1_, ...), custom_call_target="tpu_custom_call" | custom-call | tf_op jit(solution)/shard_map/finish/pallas_call | solution.py:643

commit v6 on v5

--- a/solution.py
+++ b/solution.py
@@ -165,7 +165,7 @@
         members.append((seg * ny + at, {"segment": seg, "gy": at}))
 
     barrier = pltpu.get_barrier_semaphore()
-    partners = [peer for _, peer in columns + members]
+    partners = [peer for _, peer in members + columns]
     partners += [xu, xd, {**xu, "gy": yu}, {**xd, "gy": yd}]
     for peer in partners:
         pl.semaphore_signal(barrier, inc=1, device_id=peer, device_id_type=MESH)
@@ -230,6 +230,14 @@
     loads[0].wait()
     loads[1].wait()
     lax.fori_loop(0, 8, own_plane, 0, unroll=UNROLL[0])
+
+    pl.semaphore_wait(barrier, len(partners))
+
+    c_raw = [
+        send(5 * n, v.at[:, 3, pl.ds(32 * n, 32)], halo.at[:, pl.ds(32 * n, 32)], xu) for n in range(2)
+    ]
+    c_a1y = send(1, a1.at[pl.ds(1, 4), pl.ds(1024, 48)], a1.at[pl.ds(1, 4), pl.ds(0, 48)], {"gy": yu})
+    c_a1c = send(2, a1.at[4, pl.ds(1024, 48)], a1.at[0, pl.ds(0, 48)], {**xu, "gy": yu})
 
     for load in loads[2:]:
         load.wait()
@@ -254,14 +262,6 @@
     b1 = jnp.concatenate([b1, b1], axis=0)
     bl = to_column(bl_row[...])
 
-    pl.semaphore_wait(barrier, len(partners))
-
-    c_raw = [
-        send(5 * n, v.at[:, 3, pl.ds(32 * n, 32)], halo.at[:, pl.ds(32 * n, 32)], xu) for n in range(2)
-    ]
-    c_a1y = send(1, a1.at[pl.ds(1, 4), pl.ds(1024, 48)], a1.at[pl.ds(1, 4), pl.ds(0, 48)], {"gy": yu})
-    c_a1c = send(2, a1.at[4, pl.ds(1024, 48)], a1.at[0, pl.ds(0, 48)], {**xu, "gy": yu})
-
     def conv_high(px, t):
         cols = []
         for h in range(2):
@@ -367,7 +367,8 @@
     mine = jnp.broadcast_to(jnp.sum(jnp.where(lane == row, sums, 0.0), axis=0, keepdims=True), (8, 128))
     pool_s[0] = mine
     pool_1[mx] = mine
-    spread(0, mx, columns, pool_1, lambda peer: pool_s.at[0])
+    line_1, line_2 = pool_1.at[:, pl.ds(0, 1)], pool_2.at[:, pl.ds(0, 1)]
+    spread(0, mx, columns, line_1, lambda peer: pool_s.at[0, pl.ds(0, 1)])
 
     c_sx = send(6, slope.at[0], slope.at[1], xd)
     c_sy = send(7, slope.at[0, pl.ds(0, 32)], slope_y.at[0], {"gy": yd})
@@ -416,11 +417,11 @@
 
     lax.fori_loop(0, 8, spread_own, 0, unroll=UNROLL[6])
 
-    arrive(0, pool_1, nx)
+    arrive(0, line_1, nx)
     part = add_up(pool_1, nx)
     pool_s[1] = part
     pool_2[mg] = part
-    spread(2, mg, members, pool_2, lambda peer: pool_s.at[1])
+    spread(2, mg, members, line_2, lambda peer: pool_s.at[1, pl.ds(0, 1)])
 
     c_sx.wait_recv()
     c_sy.wait_recv()
@@ -466,13 +467,14 @@
     g_2[mg] = part
     spread(3, mg, members, g_2, lambda peer: g_2s)
 
-    arrive(2, pool_2, group)
+    offset, wanted = to_column(hb_row[...]), to_column(tg_row[...])
+    arrive(2, line_2, group)
     part = add_up(pool_2, group)
     scale = 1.0 / cells
     pooled = part[0:1, 0:32] * scale
     weight = hw[...]
-    predicted = jnp.sum(weight * pooled, axis=1, keepdims=True) + to_column(hb_row[...])
-    error = predicted - to_column(tg_row[...])
+    predicted = jnp.sum(weight * pooled, axis=1, keepdims=True) + offset
+    error = predicted - wanted
     signal = jnp.sum(weight * error, axis=0, keepdims=True)
     head_out[...] = error * pooled
     pred_out[...] = jnp.sum(jnp.where(eye(4), predicted, 0.0), axis=0, keepdims=True)
@@ -560,14 +562,19 @@
 
 
 def finish(*refs):
-    sources, results, sem = refs[:7], refs[7:14], refs[14]
-    pairs = [(sources[0].at[pl.ds(4 * n, 4)], results[0].at[pl.ds(4 * n, 4)]) for n in range(4)]
-    pairs += list(zip(sources[1:], results[1:]))
-    moves = [pltpu.make_async_copy(a, b, sem.at[n]) for n, (a, b) in enumerate(pairs)]
-    for move in moves:
-        move.start()
-    for move in moves:
-        move.wait()
+    sources, results, held, come, go = refs[:7], refs[7:14], refs[14:21], refs[21], refs[22]
+    chain = [(sources[n], held[n], results[n]) for n in range(1, 7)]
+    for n in range(4):
+        chain.append([r.at[pl.ds(4 * n, 4)] for r in (sources[0], held[0], results[0])])
+    loads = [pltpu.make_async_copy(x, y, come.at[n]) for n, (x, y, _) in enumerate(chain)]
+    stores = [pltpu.make_async_copy(y, z, go.at[n]) for n, (_, y, z) in enumerate(chain)]
+    for load in loads:
+        load.start()
+    for load, store in zip(loads, stores):
+        load.wait()
+        store.start()
+    for store in stores:
+        store.wait()
 
 
 def shards(nx, ny, volume, weight_high, bias_high, weight_low, bias_low, head_weight, head_bias, targets):
@@ -582,7 +589,6 @@
         targets[None],
     )
     tables = [jnp.asarray(t(), BF) for t in (early_tables, late_tables)]
-    vm = pl.BlockSpec(memory_space=pltpu.VMEM)
     hbm = pl.BlockSpec(memory_space=pltpu.HBM)
     dma = pltpu.SemaphoreType.DMA
     per = 16 // nx
@@ -643,9 +649,9 @@
     bg, pred, head, low, low_bias, high, high_bias = pl.pallas_call(
         finish,
         out_shape=results,
-        in_specs=[vm] * 7,
+        in_specs=[hbm] * 7,
         out_specs=(hbm,) * 7,
-        scratch_shapes=[dma((10,))],
+        scratch_shapes=[*(pltpu.VMEM(x.shape, x.dtype) for x in results), dma((10,)), dma((10,))],
         compiler_params=pltpu.CompilerParams(vmem_limit_bytes=64 << 20),
         name="finish",
     )(*outs)

time: 43.6 us -> 42.6 us (0.977)
  Pallas kernels: 42.9 us -> 41.8 us
    pallas_call x1, Pallas kernels: 40.7 us -> 39.7 us  [shards(): pl.pallas_call(functools.partial(kernel, nx, ny, cells), out_shape=result...]
where the time goes in v6:
time: 42.6 us; the launch traced here: 42.4 us
  Pallas kernels  41.8 us (98%)
  between operations  0.64 us (2%)
    pallas_call x1, Pallas kernels, shards(): pl.pallas_call(functools.partial(kernel, nx, ny, cells), out_shape=result...  39.7 us
    pallas_call x1, Pallas kernels, shards(): pl.pallas_call(finish, out_shape=results, in_specs=[hbm] * 7, out_specs=(...  2.06 us

profile of v6, /device:TPU:1, one launch (start us, length us, event | category | flops | bytes accessed | tf_op | source)
XLA Modules:
  0.0 42.4 jit_solution(9332864141425933741)
XLA Ops:
  0.6 39.7 %fused.1 = (bf16[16,4,32,128]{3,2,1,0:T(8,128)(2,1)}, f32[1,4]{1,0:T(1,128)}, f32[4,32]{1,0:T(4,128)}, f32[432,32]{1,0:T(8,128)}, f32[1,32]{1,0:T(1,128)}, /*index=5*/f32[27,4,16]{2,1,0:T(4,128)}, f32[1,16]{1,0:T(1,128)}) custom-call(bf16[4,8,64,256]{3,2,1,0:T(8,128)(2,1)} %v_hbm.1, bf16[256,896]{1,0:T(8,128)(2,1)} %constant.4.clone.ta_hbm, ...), custom_call_target="tpu_custom_call" | custom-call | tf_op jit(solution)/shard_map/fused/pallas_call | solution.py:605
  40.4 2.1 %finish.1 = (bf16[16,4,32,128]{3,2,1,0:T(8,128)(2,1)}, f32[1,4]{1,0:T(1,128)}, f32[4,32]{1,0:T(4,128)}, f32[432,32]{1,0:T(8,128)}, f32[1,32]{1,0:T(1,128)}, /*index=5*/f32[27,4,16]{2,1,0:T(4,128)}, f32[1,16]{1,0:T(1,128)}) custom-call(bf16[16,4,32,128]{3,2,1,0:T(8,128)(2,1)} %get-tuple-element.21.refs_0_, f32[1,4]{1,0:T(1,128)} %get-tuple-element.22.refs_1_, ...), custom_call_target="tpu_custom_call" | custom-call | tf_op jit(solution)/shard_map/finish/pallas_call | solution.py:649

commit v7 on v6

--- a/solution.py
+++ b/solution.py
@@ -207,29 +207,27 @@
             part = part + buffer[d]
         return part
 
-    def to_channels(load, xs, yb):
+    def to_channels(rows, xs, first):
+        count = rows.shape[1] // 16
+        d = mm(rows.reshape(64 * count, 256), ta[:, 0:384]).astype(BF)
         parts = []
-        for h in range(2):
-            raw = load(yb * 2 + h).reshape(64, 256)
-            d = mm(raw, ta[:, 0:384]).astype(BF)
-            parts.append(jnp.concatenate([d[:, 0:128], d[:, 128:256], d[:, 256:384]], axis=0))
+        for h in range(count):
+            at = [16 * (c * count + h) for c in range(4)]
+            parts.append(
+                jnp.concatenate([d[r:r + 16, 128 * k:128 * (k + 1)] for k in range(3) for r in at], axis=0)
+            )
         out = mm(ta[:, 384:576], jnp.concatenate(parts, axis=1)).astype(BF)
-        for h in range(2):
-            start = pl.multiple_of(48 + (yb * 2 + h) * 256, 16)
+        for h in range(count):
+            start = pl.multiple_of(48 + (first + h) * 256, 16)
             a1[xs, pl.ds(start, 256), :] = out[:, h * 128:(h + 1) * 128]
 
     def own_plane(t, carry):
-        x, yb = t // 2, lax.rem(t, 2)
-
-        def load(b):
-            return v[:, x, pl.ds(pl.multiple_of(b * 16, 16), 16), :]
-
-        to_channels(load, x + 1, yb)
+        to_channels(v[:, t], t + 1, 0)
         return carry
 
     loads[0].wait()
     loads[1].wait()
-    lax.fori_loop(0, 8, own_plane, 0, unroll=UNROLL[0])
+    lax.fori_loop(0, 4, own_plane, 0, unroll=4)
 
     pl.semaphore_wait(barrier, len(partners))
 
@@ -330,10 +328,7 @@
         def _():
             halo[:, 32 * n:32 * n + 32, :] = jnp.zeros((4, 32, 256), BF)
 
-        def load(b):
-            return halo[:, 16 * b:16 * b + 16, :]
-
-        to_channels(load, 0, n)
+        to_channels(halo[:, 32 * n:32 * n + 32, :], 0, 2 * n)
         lax.fori_loop(4 * n, 4 * n + 4, conv_high_0, 0, unroll=UNROLL[1])
     conv_edge(0)
     all_taps(1)

time: 42.6 us -> 42.3 us (level)
  no operation moved by 1% of the time
where the time goes in v7:
time: 42.3 us; the launch traced here: 42.2 us
  Pallas kernels  41.5 us (98%)
  between operations  0.64 us (2%)
    pallas_call x1, Pallas kernels, shards(): pl.pallas_call(functools.partial(kernel, nx, ny, cells), out_shape=result...  39.5 us
    pallas_call x1, Pallas kernels, shards(): pl.pallas_call(finish, out_shape=results, in_specs=[hbm] * 7, out_specs=(...  2.06 us

profile of v7, /device:TPU:1, one launch (start us, length us, event | category | flops | bytes accessed | tf_op | source)
XLA Modules:
  0.0 42.2 jit_solution(14062395900325302194)
XLA Ops:
  0.6 39.5 %fused.1 = (bf16[16,4,32,128]{3,2,1,0:T(8,128)(2,1)}, f32[1,4]{1,0:T(1,128)}, f32[4,32]{1,0:T(4,128)}, f32[432,32]{1,0:T(8,128)}, f32[1,32]{1,0:T(1,128)}, /*index=5*/f32[27,4,16]{2,1,0:T(4,128)}, f32[1,16]{1,0:T(1,128)}) custom-call(bf16[4,8,64,256]{3,2,1,0:T(8,128)(2,1)} %v_hbm.1, bf16[256,896]{1,0:T(8,128)(2,1)} %constant.4.clone.ta_hbm, ...), custom_call_target="tpu_custom_call" | custom-call | tf_op jit(solution)/shard_map/fused/pallas_call | solution.py:600
  40.1 2.1 %finish.1 = (bf16[16,4,32,128]{3,2,1,0:T(8,128)(2,1)}, f32[1,4]{1,0:T(1,128)}, f32[4,32]{1,0:T(4,128)}, f32[432,32]{1,0:T(8,128)}, f32[1,32]{1,0:T(1,128)}, /*index=5*/f32[27,4,16]{2,1,0:T(4,128)}, f32[1,16]{1,0:T(1,128)}) custom-call(bf16[16,4,32,128]{3,2,1,0:T(8,128)(2,1)} %get-tuple-element.21.refs_0_, f32[1,4]{1,0:T(1,128)} %get-tuple-element.22.refs_1_, ...), custom_call_target="tpu_custom_call" | custom-call | tf_op jit(solution)/shard_map/finish/pallas_call | solution.py:644
